TPU v7x, 256 devices: a whole 4x4x8 slice. The times are simulated.
256 devices in a mesh: lat: 32 (over y_hi, z, core), lon: 8 (over x, y_lo).
Axes of the slice: x: 4, y: 4 (y_hi: 2, y_lo: 2; y = y_hi * 2 + y_lo), z: 8, core: 2. Of those that a mesh axis runs over, the one named last changes fastest.
Arguments:
- inputs: bfloat16 [2048, 512, 128], P('lat', 'lon'), may hold values from -6 to 6
- w_first: bfloat16 [221184], P(('lat', 'lon')), may hold values from -0.1875 to 0.1875
- w_second: bfloat16 [331776], P(('lat', 'lon')), may hold values from -0.15625 to 0.15625
- w_third: bfloat16 [331776], P(('lat', 'lon')), may hold values from -0.15625 to 0.15625
- cotangent: bfloat16 [1024, 256, 192], P('lat', 'lon'), may hold values from -6 to 6
Outputs:
- features: bfloat16 [1024, 256, 192], P('lat', 'lon')
- grad_input: bfloat16 [2048, 512, 128], P('lat', 'lon')
- grad_first: float32 [221184], P(('lat', 'lon'))
- grad_second: float32 [331776], P(('lat', 'lon'))
- grad_third: float32 [331776], P(('lat', 'lon'))
All inputs are finite; a program needn't handle non-finite values.
Results may differ from a plain program's by a relative error of at most 0.011.
Values may be sent and summed in bfloat16 or wider, within the bound.
A program may use at most 64 MiB of HBM per device.

v0:
```python
import jax
import jax.numpy as jnp
from jax import lax
from jax.sharding import PartitionSpec as P

LOSS_CELLS = 1024


LAYOUT = ("NHWC", "HWIO", "NHWC")


def padded_2(block, sides, width, periodic):
    for axis, dim in sides:
        count = lax.axis_size(axis)
        forward = [(i, i + 1) for i in range(count - 1)]
        if periodic:
            forward.append((count - 1, 0))
        backward = [(target, source) for source, target in forward]
        low = lax.ppermute(
            lax.slice_in_dim(block, block.shape[dim] - width, None, axis=dim), axis, forward
        )
        high = lax.ppermute(lax.slice_in_dim(block, 0, width, axis=dim), axis, backward)
        block = jnp.concatenate([low, block, high], axis=dim)
    return block


def passed_along(value, axis, steps):
    count = lax.axis_size(axis)
    pairs = [(source, (source + steps) % count) for source in range(count)]
    return lax.ppermute(value, axis, pairs)


def from_behind(block, axis, distance):
    devices = range(lax.axis_size(axis))
    route = [(i - distance, i) for i in devices if i - distance in devices]
    return lax.ppermute(block, axis, route)


def convolve(values, kernel, stride, padding, dilation):
    result = lax.conv_general_dilated(
        values[None],
        kernel,
        (stride, stride),
        padding,
        lhs_dilation=(dilation, dilation),
        dimension_numbers=LAYOUT,
        preferred_element_type=jnp.float32,
    )
    return result[0]


def surround(values):
    sideways = padded_2(values, (("lon", 1),), 1, True)
    return padded_2(sideways, (("lat", 0),), 1, False)


def flipped(kernel):
    return jnp.transpose(kernel[::-1, ::-1], (0, 1, 3, 2))


def derivative(preact):
    logistic = jax.nn.sigmoid(preact)
    return logistic * (1.0 + preact * (1.0 - logistic))


def kernel_grad(padded, deltas, stride, factor):
    row_count, col_count = (deltas.shape[0], deltas.shape[1])
    windows = []
    for row_tap in range(3):
        for col_tap in range(3):
            windows.append(
                padded[
                    row_tap : row_tap + stride * (row_count - 1) + 1 : stride,
                    col_tap : col_tap + stride * (col_count - 1) + 1 : stride,
                ]
            )
    columns = jnp.concatenate(windows, axis=2).reshape(row_count * col_count, -1)
    flat_deltas = deltas.reshape(row_count * col_count, -1)
    product = lax.dot_general(
        columns, flat_deltas, (((0,), (0,)), ((), ())), preferred_element_type=jnp.float32
    )
    return product.reshape(-1) * factor


def tap_term(values, kernel, row_tap, col_tap):
    return lax.dot_general(
        values,
        kernel[row_tap, col_tap],
        (((2,), (1,)), ((), ())),
        preferred_element_type=jnp.float32,
    )


def phase_spread(source, kernel, row_count, col_count):
    here = source[:row_count, :col_count]
    right = source[:row_count, 1 : col_count + 1]
    below = source[1 : row_count + 1, :col_count]
    corner = source[1 : row_count + 1, 1 : col_count + 1]
    even_even = tap_term(here, kernel, 1, 1)
    even_odd = tap_term(right, kernel, 1, 0) + tap_term(here, kernel, 1, 2)
    odd_even = tap_term(below, kernel, 0, 1) + tap_term(here, kernel, 2, 1)
    odd_odd = (
        tap_term(corner, kernel, 0, 0)
        + tap_term(below, kernel, 0, 2)
        + tap_term(right, kernel, 2, 0)
        + tap_term(here, kernel, 2, 2)
    )
    chans = even_even.shape[2]
    even_rows = jnp.stack([even_even, even_odd], axis=2).reshape(row_count, 2 * col_count, chans)
    odd_rows = jnp.stack([odd_even, odd_odd], axis=2).reshape(row_count, 2 * col_count, chans)
    return jnp.stack([even_rows, odd_rows], axis=1).reshape(2 * row_count, 2 * col_count, chans)


def local(inputs, w_first, w_second, w_third, cotangent):
    flat_one, flat_two, flat_three = (
        lax.all_gather(w_first, ("lat", "lon"), axis=0, tiled=True),
        lax.all_gather(w_second, ("lat", "lon"), axis=0, tiled=True),
        lax.all_gather(w_third, ("lat", "lon"), axis=0, tiled=True),
    )
    chan_in = inputs.shape[2]
    chan_mid = cotangent.shape[2]
    kernel_one = flat_one.reshape(3, 3, chan_in, chan_mid)
    kernel_two = flat_two.reshape(3, 3, chan_mid, chan_mid)
    kernel_three = flat_three.reshape(3, 3, chan_mid, chan_mid)
    factor = 1.0 / LOSS_CELLS
    flat_pad = ((0, 0), (0, 0))
    western = passed_along(inputs[:, -1:], "lon", 1)
    widened = jnp.concatenate([western, inputs], axis=1)
    northern = from_behind(widened[-1:], "lat", 1)
    padded_in = jnp.concatenate([northern, widened], axis=0)
    h_one = convolve(padded_in, kernel_one, 2, flat_pad, 1).astype(jnp.bfloat16)
    padded_one = surround(h_one)
    pre_two = convolve(padded_one, kernel_two, 1, flat_pad, 1)
    h_two = jax.nn.silu(pre_two).astype(jnp.bfloat16)
    padded_two = surround(h_two)
    pre_three = convolve(padded_two, kernel_three, 1, flat_pad, 1)
    features = jax.nn.silu(pre_three).astype(jnp.bfloat16)
    delta_three = (cotangent.astype(jnp.float32) * derivative(pre_three)).astype(jnp.bfloat16)
    term_three = kernel_grad(padded_two, delta_three, 1, factor)
    back_two = convolve(surround(delta_three), flipped(kernel_three), 1, flat_pad, 1)
    delta_two = (back_two * derivative(pre_two)).astype(jnp.bfloat16)
    term_two = kernel_grad(padded_one, delta_two, 1, factor)
    back_one = convolve(surround(delta_two), flipped(kernel_two), 1, flat_pad, 1).astype(
        jnp.bfloat16
    )
    term_one = kernel_grad(padded_in, back_one, 2, factor)
    half_rows, half_cols = (back_one.shape[0], back_one.shape[1])
    eastern = passed_along(back_one[:, :1], "lon", -1)
    extended = jnp.concatenate([back_one, eastern], axis=1)
    southern = from_behind(extended[:1], "lat", -1)
    extended = jnp.concatenate([extended, southern], axis=0)
    grad_input = phase_spread(extended, kernel_one, half_rows, half_cols).astype(jnp.bfloat16)
    grad_first, grad_second, grad_third = (
        lax.psum_scatter(term_one, ("lat", "lon"), scatter_dimension=0, tiled=True),
        lax.psum_scatter(term_two, ("lat", "lon"), scatter_dimension=0, tiled=True),
        lax.psum_scatter(term_three, ("lat", "lon"), scatter_dimension=0, tiled=True),
    )
    return (features, grad_input, grad_first, grad_second, grad_third)


def solution(mesh):
    placed = (
        P("lat", "lon", None),
        P(("lat", "lon")),
        P(("lat", "lon")),
        P(("lat", "lon")),
        P("lat", "lon", None),
    )
    return jax.shard_map(
        local,
        mesh=mesh,
        in_specs=placed,
        out_specs=(
            P("lat", "lon", None),
            P("lat", "lon", None),
            P(("lat", "lon")),
            P(("lat", "lon")),
            P(("lat", "lon")),
        ),
        check_vma=False,
    )
```

profile of v0, /device:TPU:2, one launch (start us, length us, event | category | flops | bytes accessed | tf_op | source)
XLA Modules:
  0.0 681.2 jit_solution(17751275319094550254)
XLA Ops:
  12.6 9.7 %slice.223 = bf16[32,32,128]{2,1,0:T(8,128)(2,1)} slice(bf16[64,64,128]{2,1,0:T(8,128)(2,1)S(1)} %copy-done), slice={[0:63:2], [0:63:2], [0:128:1]} | slice | bytes 524288 | tf_op jit(solution)/shard_map/slice | solution.py:72
  22.4 9.7 %slice.224 = bf16[32,32,128]{2,1,0:T(8,128)(2,1)} slice(bf16[64,64,128]{2,1,0:T(8,128)(2,1)S(1)} %copy-done), slice={[0:63:2], [1:64:2], [0:128:1]} | slice | bytes 524288 | tf_op jit(solution)/shard_map/slice | solution.py:72
  32.1 9.8 %slice.226 = bf16[32,32,128]{2,1,0:T(8,128)(2,1)} slice(bf16[64,64,128]{2,1,0:T(8,128)(2,1)S(1)} %copy-done), slice={[1:64:2], [0:63:2], [0:128:1]} | slice | bytes 524288 | tf_op jit(solution)/shard_map/slice | solution.py:72
  41.9 9.8 %slice.227 = bf16[32,32,128]{2,1,0:T(8,128)(2,1)} slice(bf16[64,64,128]{2,1,0:T(8,128)(2,1)S(1)} %copy-done), slice={[1:64:2], [1:64:2], [0:128:1]} | slice | bytes 524288 | tf_op jit(solution)/shard_map/slice | solution.py:72
  53.7 9.8 %slice.222 = bf16[32,32,128]{2,1,0:T(8,128)(2,1)} slice(bf16[64,65,128]{2,1,0:T(8,128)(2,1)S(1)} %pad_maximum_fusion), slice={[0:63:2], [0:63:2], [0:128:1]} | slice | bytes 524288 | tf_op jit(solution)/shard_map/slice | solution.py:72
  63.5 9.8 %slice.225 = bf16[32,32,128]{2,1,0:T(8,128)(2,1)} slice(bf16[64,65,128]{2,1,0:T(8,128)(2,1)S(1)} %pad_maximum_fusion), slice={[1:64:2], [0:63:2], [0:128:1]} | slice | bytes 524288 | tf_op jit(solution)/shard_map/slice | solution.py:72
  75.5 9.7 %slice.220 = bf16[32,32,128]{2,1,0:T(8,128)(2,1)} slice(bf16[65,65,128]{2,1,0:T(8,128)(2,1)S(1)} %get-tuple-element.11), slice={[0:63:2], [1:64:2], [0:128:1]} | slice | bytes 524288 | tf_op jit(solution)/shard_map/slice | solution.py:72
  85.2 9.7 %slice.221 = bf16[32,32,128]{2,1,0:T(8,128)(2,1)} slice(bf16[65,65,128]{2,1,0:T(8,128)(2,1)S(1)} %get-tuple-element.11), slice={[0:63:2], [2:65:2], [0:128:1]} | slice | bytes 524288 | tf_op jit(solution)/shard_map/slice | solution.py:72
  101.5 177.0 %all-reduce.13.cloned.1.call-done = (bf16[331776]{0:T(1024)(128)(2,1)}, bf16[331776]{0:T(1024)(128)(2,1)}, bf16[221184]{0:T(1024)(128)(2,1)}) async-done(((bf16[331776]{0:T(1024)(128)(2,1)}, bf16[331776]{0:T(1024)(128)(2,1)}, bf16[221184]{0:T(1024)(128)(2,1)}), (bf16[331776]{0:T(1024)(128)(2,1)}, bf16[331776]{0:T(1024)(128)(2,1)}, bf16[221184]{0:T(1024)(128)(2,1)})) %all-reduce.13.cloned.1.call-update) | async-done | bytes 1769488
  289.5 3.2 collective-permute-start.4
  299.5 2.2 fusion.92
  301.7 6.9 %concatenate.94 = bf16[32,32,1728]{2,1,0:T(8,128)(2,1)} concatenate(bf16[32,32,192]{2,1,0:T(8,128)(2,1)} %get-tuple-element.51, bf16[32,32,192]{2,1,0:T(8,128)(2,1)} %get-tuple-element.52, bf16[32,32,192]{2,1,0:T(8,128)(2,1)} %get-tuple-element.53, bf16[32,32,192]{2,1,0:T(8,128)(2,1)S(1)} %get-tuple-element.42, bf16[32,32,192]{2,1,0:T(8,128)(2,1)S(1)} %bitcast.160, ...), dimensions={2} | concatenate | bytes 7077888 | tf_op jit(solution)/shard_map/concatenate | solution.py:77
  309.9 3.0 collective-permute-start.8
  320.2 3.2 collective-permute-start.11
  324.9 3.2 collective-permute-done.10
  329.5 3.0 collective-permute-start.12
  332.5 2.3 fusion.90
  334.8 6.9 %concatenate.99 = bf16[32,32,1728]{2,1,0:T(8,128)(2,1)} concatenate(bf16[32,32,192]{2,1,0:T(8,128)(2,1)} %get-tuple-element.54, bf16[32,32,192]{2,1,0:T(8,128)(2,1)} %get-tuple-element.55, bf16[32,32,192]{2,1,0:T(8,128)(2,1)} %get-tuple-element.56, bf16[32,32,192]{2,1,0:T(8,128)(2,1)S(1)} %get-tuple-element.40, bf16[32,32,192]{2,1,0:T(8,128)(2,1)S(1)} %multiply_convert_fusion.2, ...), dimensions={2} | concatenate | bytes 7077888 | tf_op jit(solution)/shard_map/concatenate | solution.py:77
  347.2 2.4 collective-permute-start.15
  356.9 6.0 collective-permute-start.16
  362.9 4.1 fusion.2
  379.5 4.2 collective-permute-start.18
  383.8 3.4 fusion.3
  398.7 271.1 %all-reduce.11.cloned.1.call-done = (f32[221184]{0:T(1024)}, f32[331776]{0:T(1024)}, f32[331776]{0:T(1024)}) async-done(((f32[221184]{0:T(1024)}, f32[331776]{0:T(1024)}, f32[331776]{0:T(1024)}), (f32[221184]{0:T(1024)}, f32[331776]{0:T(1024)}, f32[331776]{0:T(1024)})) %all-reduce.11.cloned.1.call-update) | async-done | bytes 3538960
  (195 shorter events, 85.6 us)
Async XLA Ops:
  7.2 271.3 %all-reduce.13.cloned.1.call-start = ((), (), s32[]{:S(2)}) async-start(), calls=%async_computation.1 | async-start | bytes 3538944
  8.2 43.5 %collective-permute-start = (bf16[64,1,128]{2,1,0:T(2,128)(2,1)S(1)}, bf16[64,1,128]{2,1,0:T(2,128)(2,1)S(1)}, u32[]{:S(2)}, u32[]{:S(2)}) collective-permute-start(bf16[64,1,128]{2,1,0:T(2,128)(2,1)S(1)} %slice.187), channel_id=1, source_target_pairs={{0,1},{1,2},{2,3},{3,4},{4,5},{5,6},{6,7},{7,0},{8,9},{9,10},{10,1... | collective-permute-start | bytes 49160 | tf_op jit(solution)/shard_map/ppermute | solution.py:30
  12.2 657.5 %all-reduce.11.cloned.1.call-start = ((), (), s32[]{:S(2)}) async-start(), calls=%async_computation | async-start | bytes 7077888
  51.7 21.6 %collective-permute-start.1 = (bf16[1,65,128]{2,1,0:T(8,128)(2,1)S(1)}, bf16[1,65,128]{2,1,0:T(8,128)(2,1)S(1)}, u32[]{:S(2)}, u32[]{:S(2)}) collective-permute-start(bf16[1,65,128]{2,1,0:T(8,128)(2,1)S(1)} %fusion.71), channel_id=1, source_target_pairs={{0,8},{8,16},{16,24},{24,32},{32,40},{40,48},{48,56},{56,64},{64,7... | collective-permute-start | bytes 49928 | tf_op jit(solution)/shard_map/ppermute | solution.py:36
  99.2 180.7 %copy-start.25 = (pred[8,5]{0,1:T(8,128)(4,1)S(1)}, pred[8,5]{0,1:T(8,128)(4,1)}, u32[]{:S(2)}) copy-start(pred[8,5]{0,1:T(8,128)(4,1)} %constant.31) | copy-start | bytes 124
  281.6 4.8 collective-permute-start.3
  283.3 4.8 collective-permute-start.2
  286.3 7.8 %copy-start.15 = (bf16[3,3,192,192]{3,2,1,0:T(8,128)(2,1)}, bf16[3,3,192,192]{3,2,1,0:T(8,128)(2,1)S(1)}, u32[]{:S(2)}) copy-start(bf16[3,3,192,192]{3,2,1,0:T(8,128)(2,1)S(1)} %reshape.43) | copy-start | bytes 1990660
  288.2 5.0 collective-permute-start.5
  289.5 3.9 collective-permute-start.4
  296.9 11.7 %collective-permute-start.7 = (bf16[32,1,192]{2,1,0:T(2,128)(2,1)S(1)}, bf16[32,1,192]{2,1,0:T(2,128)(2,1)S(1)}, u32[]{:S(2)}, u32[]{:S(2)}) collective-permute-start(bf16[32,1,192]{2,1,0:T(2,128)(2,1)S(1)} %get-tuple-element.48), channel_id=1, source_target_pairs={{1,0},{2,1},{3,2},{4,3},{5,4},{6,5},{7,6},{0,7},{9,8},{10,9},{11,1... | collective-permute-start | bytes 36872 | tf_op jit(solution)/shard_map/ppermute | solution.py:22
  297.8 10.8 %collective-permute-start.6 = (bf16[32,1,192]{2,1,0:T(2,128)(2,1)S(1)}, bf16[32,1,192]{2,1,0:T(2,128)(2,1)S(1)}, u32[]{:S(2)}, u32[]{:S(2)}) collective-permute-start(bf16[32,1,192]{2,1,0:T(2,128)(2,1)S(1)} %get-tuple-element.47), channel_id=1, source_target_pairs={{0,1},{1,2},{2,3},{3,4},{4,5},{5,6},{6,7},{7,0},{8,9},{9,10},{10,1... | collective-permute-start | bytes 36872 | tf_op jit(solution)/shard_map/ppermute | solution.py:19
  308.6 4.8 collective-permute-start.9
  309.9 3.9 collective-permute-start.8
  320.2 4.8 collective-permute-start.11
  323.3 4.8 collective-permute-start.10
  328.2 13.5 %collective-permute-start.13 = (bf16[1,34,192]{2,1,0:T(8,128)(2,1)S(1)}, bf16[1,34,192]{2,1,0:T(8,128)(2,1)S(1)}, u32[]{:S(2)}, u32[]{:S(2)}) collective-permute-start(bf16[1,34,192]{2,1,0:T(8,128)(2,1)S(1)} %get-tuple-element.34), channel_id=1, source_target_pairs={{8,0},{16,8},{24,16},{32,24},{40,32},{48,40},{56,48},{64,56},{72,6... | collective-permute-start | bytes 39176 | tf_op jit(solution)/shard_map/ppermute | solution.py:22
  329.5 12.2 %collective-permute-start.12 = (bf16[1,34,192]{2,1,0:T(8,128)(2,1)S(1)}, bf16[1,34,192]{2,1,0:T(8,128)(2,1)S(1)}, u32[]{:S(2)}, u32[]{:S(2)}) collective-permute-start(bf16[1,34,192]{2,1,0:T(8,128)(2,1)S(1)} %get-tuple-element.33), channel_id=1, source_target_pairs={{0,8},{8,16},{16,24},{24,32},{32,40},{40,48},{48,56},{56,64},{64,7... | collective-permute-start | bytes 39176 | tf_op jit(solution)/shard_map/ppermute | solution.py:19
  347.2 8.3 %collective-permute-start.15 = (bf16[32,1,192]{2,1,0:T(2,128)(2,1)S(1)}, bf16[32,1,192]{2,1,0:T(2,128)(2,1)S(1)}, u32[]{:S(2)}, u32[]{:S(2)}) collective-permute-start(bf16[32,1,192]{2,1,0:T(2,128)(2,1)S(1)} %get-tuple-element.44), channel_id=1, source_target_pairs={{1,0},{2,1},{3,2},{4,3},{5,4},{6,5},{7,6},{0,7},{9,8},{10,9},{11,1... | collective-permute-start | bytes 36872 | tf_op jit(solution)/shard_map/ppermute | solution.py:22
  349.6 5.9 collective-permute-start.14
  355.6 15.2 %collective-permute-start.17 = (bf16[1,34,192]{2,1,0:T(8,128)(2,1)S(1)}, bf16[1,34,192]{2,1,0:T(8,128)(2,1)S(1)}, u32[]{:S(2)}, u32[]{:S(2)}) collective-permute-start(bf16[1,34,192]{2,1,0:T(8,128)(2,1)S(1)} %get-tuple-element.32), channel_id=1, source_target_pairs={{8,0},{16,8},{24,16},{32,24},{40,32},{48,40},{56,48},{64,56},{72,6... | collective-permute-start | bytes 39176 | tf_op jit(solution)/shard_map/ppermute | solution.py:22
  356.9 13.9 %collective-permute-start.16 = (bf16[1,34,192]{2,1,0:T(8,128)(2,1)S(1)}, bf16[1,34,192]{2,1,0:T(8,128)(2,1)S(1)}, u32[]{:S(2)}, u32[]{:S(2)}) collective-permute-start(bf16[1,34,192]{2,1,0:T(8,128)(2,1)S(1)} %get-tuple-element.31), channel_id=1, source_target_pairs={{0,8},{8,16},{16,24},{24,32},{32,40},{40,48},{48,56},{56,64},{64,7... | collective-permute-start | bytes 39176 | tf_op jit(solution)/shard_map/ppermute | solution.py:19
  379.5 12.2 %collective-permute-start.18 = (bf16[32,1,192]{2,1,0:T(2,128)(2,1)S(1)}, bf16[32,1,192]{2,1,0:T(2,128)(2,1)S(1)}, u32[]{:S(2)}, u32[]{:S(2)}) collective-permute-start(bf16[32,1,192]{2,1,0:T(2,128)(2,1)S(1)} %slice.275), channel_id=1, source_target_pairs={{0,7},{1,0},{2,1},{3,2},{4,3},{5,4},{6,5},{7,6},{8,15},{9,8},{10,9... | collective-permute-start | bytes 36872 | tf_op jit(solution)/shard_map/ppermute | solution.py:30
  391.8 4.0 collective-permute-start.19
  (24 other events, 53.7 us)
Sparse Core Ops, SparseCore 0:
  14.4 264.0 all-reduce.12
  390.4 279.2 all-reduce.10
where the time goes:
time: 690 us; the launch traced here: 681 us
  waiting for transfers between devices  457 us (66%)
  local copies, waits for them, and re-layouts  138 us (20%)
  starting transfers between devices  38.9 us (6%)
  matrix products  23.6 us (3%)
  between operations  15.3 us (2%)
  other arithmetic  8.46 us (1%)
    unnamed x4, waiting for transfers between devices  448 us
    slice x11, local copies, waits for them, and re-layouts, kernel_grad(): padded[row_tap:row_tap + stride * (row_count - 1) + 1:stride, col_tap:col...  83.4 us
    unnamed x76, local copies, waits for them, and re-layouts  19.5 us
    ppermute x8, starting transfers between devices, padded_2(): lax.ppermute(lax.slice_in_dim(block, block.shape[dim] - width, None, axis...  16.8 us
    concatenate x3, local copies, waits for them, and re-layouts, kernel_grad(): jnp.concatenate(windows, axis=2).reshape(row_count * col_count, -1)  14.5 us
  transfers between devices with their start and end apart: 22, of which 8 were waited for; matrix products, arithmetic and copies ran while one was open for 20% of the time, Pallas kernels for 0%

commit v1 on v0

v1 whole, which is shorter than its diff:
```python
import functools
import jax, jax.numpy as jnp
from jax import lax
from jax.experimental import pallas as pl
from jax.experimental.pallas import tpu as pltpu
from jax.sharding import PartitionSpec as P

LOSS_CELLS = 1024
F32, BF16 = jnp.float32, jnp.bfloat16
W = 48
def mm(a, b):
    return lax.dot_general(a, b, (((1,), (0,)), ((), ())), preferred_element_type=F32)
def mmt(a, b):
    return lax.dot_general(a, b, (((1,), (1,)), ((), ())), preferred_element_type=F32)

def compute_kernel(lat_ref, x_ref, xe_ref, xw_ref, xn_ref, xs_ref, c_ref, ce_ref, cw_ref, cn_ref, cs_ref, w_ref,
                   feat_ref, gin_ref, gb_ref,
                   xf, x0, x1, kf, k1, k2, k3, cf, hs1, hs2, ds3, ds2, bs, p2, dt, g1, g23, st, of, il):
    lat = lat_ref[0]
    last = lat_ref[1]
    for g in range(32):
        v = w_ref[g].astype(F32)
        kf[54 * g : 54 * g + 54, :] = v[0:54]
        of[36 * g : 36 * g + 18, :] = v[54:72, 0:192]
        of[36 * g + 18 : 36 * g + 36, :] = v[54:72, 192:384]
    k1[...] = of[0:1152, :].astype(BF16)
    k2[...] = kf[:, 0:192].astype(BF16)
    k3[...] = kf[:, 192:384].astype(BF16)
    north = (lat > 0).astype(F32)
    south = (lat < last).astype(F32)

    def put_row(p, own, east, west, scale):
        slot = lax.rem(p, 2)
        row = xf.at[slot]
        own, east, west = own.astype(F32) * scale, east.astype(F32) * scale, west.astype(F32) * scale
        row[8:72, :] = own
        row[72:88, :] = east
        row[88:104, :] = west
        row[0:8, :] = west[8:16]
    def split_row(slot, dst, idx):
        row = xf.at[slot]
        dst[idx, :, 0:128] = row[pl.ds(7, W, stride=2), :].astype(BF16)
        dst[idx, :, 128:256] = row[pl.ds(8, W, stride=2), :].astype(BF16)
        dst[idx, :, 256:384] = row[pl.ds(9, W, stride=2), :].astype(BF16)
    def own_rows(k, _):
        r = 2 * k
        for d in range(2):
            slot = (9 + d) % 2
            put_row(slot, x_ref[r + d], xe_ref[r + d], xw_ref[r + d], 1.0)
        split_row(1, x1, k + 4)
        split_row(0, x0, k + 5)
        return 0
    lax.fori_loop(0, 32, own_rows, 0)
    for q in range(1, 10):
        p = q - 1
        put_row(p % 2, xn_ref[q, 0:64], xn_ref[q, 64:80], xn_ref[q, 80:96], north)
        split_row(p % 2, x0 if p % 2 == 0 else x1, p // 2)
    for q in range(10):
        p = 73 + q
        put_row(p % 2, xs_ref[q, 0:64], xs_ref[q, 64:80], xs_ref[q, 80:96], south)
        split_row(p % 2, x0 if p % 2 == 0 else x1, p // 2)

    def cot(idx, row, east, west):
        cf[idx, 0:32, :] = row.astype(F32)
        cf[idx, 32:40, :] = east[0:8].astype(F32)
        cf[idx, 40:48, :] = west[8:16].astype(F32)
    def cot_own(k, _):
        cot(k + 2, c_ref[k], ce_ref[k].astype(F32), cw_ref[k].astype(F32))
        return 0
    lax.fori_loop(0, 32, cot_own, 0)
    for q in range(2):
        v = cn_ref[q + 1].astype(F32)
        cot(q, v[0:32], v[32:48], v[48:64])
    for q in range(3):
        v = cs_ref[q].astype(F32)
        cot(q + 34, v[0:32], v[32:48], v[48:64])

    def rows_ok(start, n, first):
        i = lax.broadcasted_iota(jnp.int32, (n, W, 192), 0) + (start + first)
        glob = i + 32 * lat
        return (glob >= 0) & (glob < 32 * (last + 1))
    def put_shifted(dst, start, n, value):
        dst[1, pl.ds(start, n)] = value.astype(BF16)
        dst[0, pl.ds(start, n)] = pltpu.roll(value, 1, 1).astype(BF16)
        dst[2, pl.ds(start, n)] = pltpu.roll(value, W - 1, 1).astype(BF16)
    def chunks(total, n, body):
        count = -(-total // n)
        def step(k, _):
            body(jnp.minimum(k * n, total - n))
            return 0
        lax.fori_loop(0, count, step, 0)

    def h_one(s):
        n = 14
        acc = mm(x0[pl.ds(s, n)].reshape(n * W, 384), k1[0:384])
        acc += mm(x1[pl.ds(s, n)].reshape(n * W, 384), k1[384:768])
        acc += mm(x0[pl.ds(s + 1, n)].reshape(n * W, 384), k1[768:1152])
        v = jnp.where(rows_ok(s, n, -4), acc.reshape(n, W, 192), 0.0)
        put_shifted(hs1, s, n, v)
    chunks(41, 14, h_one)

    def conv(src, k, s, n):
        acc = None
        for a in range(3):
            for b in range(3):
                t = mm(src[b, pl.ds(s + a, n)].reshape(n * W, 192), k[(3 * a + b) * 192 : (3 * a + b + 1) * 192])
                acc = t if acc is None else acc + t
        return acc.reshape(n, W, 192)
    def tconv(src, k, s, n):
        acc = None
        for a in range(3):
            for b in range(3):
                t = mmt(src[2 - b, pl.ds(s + 2 - a, n)].reshape(n * W, 192), k[(3 * a + b) * 192 : (3 * a + b + 1) * 192])
                acc = t if acc is None else acc + t
        return acc.reshape(n, W, 192)

    def h_two(s):
        n = 13
        v = conv(hs1, k2, s, n)
        p2[pl.ds(s, n)] = v
        h = v / (1.0 + jnp.exp(-v))
        put_shifted(hs2, s, n, jnp.where(rows_ok(s, n, -3), h, 0.0))
    chunks(39, 13, h_two)

    def deriv(v):
        sg = 1.0 / (1.0 + jnp.exp(-v))
        return sg, sg * (1.0 + v * (1.0 - sg))
    ft = bs
    def d_three(s):
        n = 13
        v = conv(hs2, k3, s, n)
        sg, dv = deriv(v)
        ft[1, pl.ds(s, n)] = (v * sg).astype(BF16)
        d = jnp.where(rows_ok(s, n, -2), cf[pl.ds(s, n)] * dv, 0.0)
        put_shifted(ds3, s, n, d)
    chunks(37, 13, d_three)
    feat_ref[...] = ft[1, 2:34, 0:32, :]

    def wgrad(src, off, dst, lo):
        for a in range(3):
            for b in range(3):
                win = src[b, off + a : off + a + 32, 0:32, :].reshape(1024, 192)
                t = mm(dt[...], win)
                n0 = (3 * a + b) * 192
                dst[n0 : n0 + 192, lo : lo + 192] = t.T
    dt[...] = ds3[1, 2:34, 0:32, :].reshape(1024, 192).T
    wgrad(hs2, 2, g23, 192)

    def d_two(s):
        n = 12
        v = tconv(ds3, k3, s, n)
        _, dv = deriv(p2[pl.ds(s + 2, n)])
        d = jnp.where(rows_ok(s, n, -1), v * dv, 0.0)
        put_shifted(ds2, s, n, d)
    chunks(35, 12, d_two)
    dt[...] = ds2[1, 1:33, 0:32, :].reshape(1024, 192).T
    wgrad(hs1, 3, g23, 0)

    def b_one(s):
        n = 11
        v = tconv(ds2, k2, s, n)
        v = jnp.where(rows_ok(s, n, 0), v, 0.0)
        bs[1, pl.ds(s, n)] = v.astype(BF16)
        bs[2, pl.ds(s, n)] = pltpu.roll(v, W - 1, 1).astype(BF16)
    chunks(33, 11, b_one)
    dt[...] = bs[1, 0:32, 0:32, :].reshape(1024, 192).T
    for a in range(3):
        src = x1 if a == 1 else x0
        off = 4 + (a == 2)
        win = src[off : off + 32, 0:32, :].reshape(1024, 384)
        t = mm(dt[...], win)
        g1[384 * a : 384 * a + 384, :] = t.T

    for g in range(32):
        st[0:54, :] = g23[54 * g : 54 * g + 54, :]
        st[54:72, 0:192] = g1[36 * g : 36 * g + 18, :]
        st[54:72, 192:384] = g1[36 * g + 18 : 36 * g + 36, :]
        gb_ref[g] = st[...].astype(BF16)

    def k1t(a, b):
        n0 = (3 * a + b) * 128
        return k1[n0 : n0 + 128]
    def gin(s):
        n = 8
        i = s
        here = bs[1, pl.ds(i, n), 0:32, :].reshape(n * 32, 192)
        right = bs[2, pl.ds(i, n), 0:32, :].reshape(n * 32, 192)
        below = bs[1, pl.ds(i + 1, n), 0:32, :].reshape(n * 32, 192)
        corner = bs[2, pl.ds(i + 1, n), 0:32, :].reshape(n * 32, 192)
        ee = mmt(here, k1t(1, 1))
        eo = mmt(right, k1t(1, 0)) + mmt(here, k1t(1, 2))
        oe = mmt(below, k1t(0, 1)) + mmt(here, k1t(2, 1))
        oo = mmt(corner, k1t(0, 0)) + mmt(below, k1t(0, 2)) + mmt(right, k1t(2, 0)) + mmt(here, k1t(2, 2))
        il[pl.ds(0, n * 32, stride=2), :] = ee
        il[pl.ds(1, n * 32, stride=2), :] = eo
        il[pl.ds(n * 64, n * 32, stride=2), :] = oe
        il[pl.ds(n * 64 + 1, n * 32, stride=2), :] = oo
        even = il[0 : n * 64, :].reshape(n, 64, 128).astype(BF16)
        odd = il[n * 64 : n * 128, :].reshape(n, 64, 128).astype(BF16)
        for m in range(n):
            gin_ref[2 * (i + m)] = even[m]
            gin_ref[2 * (i + m) + 1] = odd[m]
    chunks(32, 8, gin)

def compute(lat2, x, xe, xw, xn, xs, c, ce, cw, cn, cs, w):
    V = pltpu.VMEM
    vm = pl.BlockSpec(memory_space=pltpu.VMEM)
    return pl.pallas_call(
        compute_kernel,
        out_shape=(jax.ShapeDtypeStruct((32, 32, 192), BF16), jax.ShapeDtypeStruct((64, 64, 128), BF16),
                   jax.ShapeDtypeStruct((32, 72, 384), BF16)),
        in_specs=[pl.BlockSpec(memory_space=pltpu.SMEM)] + [vm] * 11,
        out_specs=(vm, vm, vm),
        scratch_shapes=[
            V((2, 104, 128), F32), V((42, W, 384), BF16), V((42, W, 384), BF16),
            V((1728, 384), F32), V((1152, 192), BF16), V((1728, 192), BF16), V((1728, 192), BF16),
            V((37, W, 192), F32), V((3, 41, W, 192), BF16), V((3, 39, W, 192), BF16),
            V((3, 37, W, 192), BF16), V((3, 35, W, 192), BF16), V((3, 37, W, 192), BF16),
            V((39, W, 192), F32), V((192, 1024), BF16), V((1152, 192), F32), V((1728, 384), F32), V((72, 384), F32),
            V((1152, 192), F32), V((1024, 128), F32),
        ],
        compiler_params=pltpu.CompilerParams(vmem_limit_bytes=60 * 1024 * 1024),
        cost_estimate=pl.CostEstimate(flops=8_000_000_000, bytes_accessed=8_000_000, transcendentals=0),
        name="level_compute",
    )(lat2, x, xe, xw, xn, xs, c, ce, cw, cn, cs, w)


MESH = pl.DeviceIdType.MESH
LON, ZS, GROUPS = 8, 8, 32
S1, S2 = 864, 1296


def pieces(size, base_row, base_lane, per_row):
    out = []
    total = size * LON
    for row in range(total // 192):
        at = row * 192
        while at < (row + 1) * 192:
            shard = at // size
            end = min((row + 1) * 192, (shard + 1) * size)
            lane = at - row * 192
            out.append((shard, at - shard * size, row, lane, end - at))
            at = end
    return out


def group_map():
    moves = []
    for shard, lane, row, at, n in pieces(S1, 0, 0, 0):
        moves.append((shard, lane, 54 + row % 18, 192 * (row // 18) + at, n))
    for k in range(2):
        for shard, lane, row, at, n in pieces(S2, 0, 0, 0):
            moves.append((shard, S1 + k * S2 + lane, row, 192 * k + at, n))
    return moves


def place():
    lat, lon = lax.axis_index("lat"), lax.axis_index("lon")
    core = lax.rem(lat, 2)
    z = lax.rem(lax.div(lat, 2), ZS)
    yh = lax.div(lat, 2 * ZS)
    return lat, lon, yh, z, core


def barrier(peers):
    sem = pltpu.get_barrier_semaphore()
    for peer in peers:
        pl.semaphore_signal(sem, inc=1, device_id=peer, device_id_type=MESH)
    pl.semaphore_wait(sem, len(peers))


def gather_kernel(v_ref, x_ref, c_ref, xe, xw, xn, xs, ce, cw, cn, cs, wb,
                  vbuf, stage, own, vsend, vrecv, hsend, hrecv, wsend, wrecv, osem):
    lat, lon, yh, z, core = place()
    east, west = lax.rem(lon + 1, LON), lax.rem(lon + LON - 1, LON)
    north, south = lax.rem(lat + 31, 32), lax.rem(lat + 1, 32)
    partner = lat + 1 - 2 * core
    across = lax.rem(lat + 16, 32)
    def at_z(k):
        return yh * 16 + lax.rem(z + k + ZS, ZS) * 2 + core
    lons = [lax.rem(lon + d, LON) for d in range(1, LON)]
    barrier([(lat, p) for p in lons] + [(q, lon) for q in (north, south, across, at_z(1), at_z(-1))])

    def remote(src, dst, send, recv, peer):
        return pltpu.make_async_remote_copy(src_ref=src, dst_ref=dst, send_sem=send, recv_sem=recv,
                                            device_id=peer, device_id_type=MESH)
    vs = []
    for d in range(1, LON):
        k = remote(v_ref, vbuf.at[lon], vsend.at[d], vrecv.at[lon], (lat, lons[d - 1]))
        k.start()
        vs.append(k)
    halos = []
    def halo(src, dst, peer):
        n = len(halos)
        k = remote(src, dst, hsend.at[n], hrecv.at[n], peer)
        k.start()
        halos.append(k)
    e, w, n, s = (lat, east), (lat, west), (north, lon), (south, lon)
    halo(x_ref.at[:, 0:16], xe, w)
    halo(x_ref.at[:, 48:64], xw, e)
    halo(c_ref.at[:, 0:16], ce, w)
    halo(c_ref.at[:, 16:32], cw, e)
    halo(x_ref.at[54:64], xn.at[:, 0:64], s)
    halo(x_ref.at[0:10], xs.at[:, 0:64], n)
    halo(c_ref.at[29:32], cn.at[:, 0:32], s)
    halo(c_ref.at[0:3], cs.at[:, 0:32], n)

    vbuf[lon] = v_ref[...]
    for d in range(1, LON):
        src = lons[d - 1]
        remote(v_ref, vbuf.at[src], vsend.at[d], vrecv.at[src], (lat, src)).wait_recv()
    for shard, lane, row, at, length in group_map():
        stage[row : row + 1, at : at + length] = vbuf[shard, :, lane : lane + length]
    own[...] = stage[...].astype(BF16)

    started = []
    def send(src, slot, peer):
        k = remote(src, wb.at[slot], wsend.at[len(started)], wrecv.at[slot], peer)
        k.start()
        started.append(k)
    def arrived(slot):
        remote(own, wb.at[slot], wsend.at[0], wrecv.at[slot], (partner, lon)).wait_recv()
    up, down = (at_z(1), lon), (at_z(-1), lon)
    mine = pltpu.make_async_copy(own, wb.at[lat], osem)
    mine.start()
    send(own, lat, up)
    send(own, lat, down)
    send(own, lat, (across, lon))
    send(own, lat, (partner, lon))

    for k in range(4):
        halos[k].wait_recv()
    halo(xe.at[54:64], xn.at[:, 64:80], s)
    halo(xw.at[54:64], xn.at[:, 80:96], s)
    halo(xe.at[0:10], xs.at[:, 64:80], n)
    halo(xw.at[0:10], xs.at[:, 80:96], n)
    halo(ce.at[29:32], cn.at[:, 32:48], s)
    halo(cw.at[29:32], cn.at[:, 48:64], s)
    halo(ce.at[0:3], cs.at[:, 32:48], n)
    halo(cw.at[0:3], cs.at[:, 48:64], n)

    def slot_of(half, k):
        return half * 16 + lax.rem(z + k + ZS, ZS) * 2 + core
    other = 1 - yh
    second = slot_of(other, 0)
    def pass_on(half, t, sign, last):
        slot = slot_of(half, -sign * t)
        arrived(slot)
        if t < last:
            send(wb.at[slot], slot, up if sign > 0 else down)
        send(wb.at[slot], slot, (partner, lon))
    for t in range(0, 5):
        if t >= 1:
            if t <= 4:
                pass_on(yh, t, 1, 4)
            if t <= 3:
                pass_on(yh, t, -1, 3)
        if t == 0:
            arrived(second)
            send(wb.at[second], second, up)
            send(wb.at[second], second, down)
            send(wb.at[second], second, (partner, lon))
        else:
            if t <= 3:
                pass_on(other, t, 1, 3)
            if t <= 4:
                pass_on(other, t, -1, 4)
    for half in range(2):
        for k in range(ZS):
            arrived(half * 16 + k * 2 + 1 - core)
    mine.wait()
    for k in started:
        k.wait_send()
    for k in vs:
        k.wait_send()
    for n, k in enumerate(halos):
        k.wait_send()
        if n >= 4:
            k.wait_recv()


def gather(v, x, c):
    anyspec = pl.BlockSpec(memory_space=pl.ANY)
    sds = jax.ShapeDtypeStruct
    return pl.pallas_call(
        gather_kernel,
        out_shape=(sds((64, 16, 128), BF16), sds((64, 16, 128), BF16), sds((10, 96, 128), BF16), sds((10, 96, 128), BF16),
                   sds((32, 16, 192), BF16), sds((32, 16, 192), BF16), sds((3, 64, 192), BF16), sds((3, 64, 192), BF16),
                   sds((32, 72, 384), BF16)),
        in_specs=[pl.BlockSpec(memory_space=pltpu.VMEM), anyspec, anyspec],
        out_specs=(anyspec,) * 9,
        scratch_shapes=[
            pltpu.VMEM((LON, 1, 3456), F32), pltpu.VMEM((72, 384), F32), pltpu.VMEM((72, 384), BF16),
            pltpu.SemaphoreType.DMA((LON,)), pltpu.SemaphoreType.DMA((LON,)),
            pltpu.SemaphoreType.DMA((16,)), pltpu.SemaphoreType.DMA((16,)),
            pltpu.SemaphoreType.DMA((34,)), pltpu.SemaphoreType.DMA((GROUPS,)), pltpu.SemaphoreType.DMA,
        ],
        compiler_params=pltpu.CompilerParams(collective_id=0, has_side_effects=True),
        name="gather_weights",
    )(v, x, c)


def reduce_kernel(gb, o1, o2, o3, r1, sbuf, r2, acc, own3, r3, blk, pbuf, r4,
                  a_send, a_recv, z_send, z_recv, y_sem, l_send, l_recv):
    lat, lon, yh, z, core = place()
    partner = lat + 1 - 2 * core
    across = lax.rem(lat + 16, 32)
    lons = [lax.rem(lon + d, LON) for d in range(1, LON)]
    zs = [lax.rem(z + d, ZS) for d in range(ZS)]
    def lat_of(zz):
        return yh * 16 + zz * 2 + core
    barrier([(lat, p) for p in lons] + [(partner, lon), (across, lon)] + [(lat_of(zz), lon) for zz in zs[1:]])

    def remote(src, dst, send, recv, peer):
        return pltpu.make_async_remote_copy(src_ref=src, dst_ref=dst, send_sem=send, recv_sem=recv,
                                            device_id=peer, device_id_type=MESH)
    order = (4, 3, 5, 2, 6, 1, 7, 0)
    first = []
    for d in order:
        zz = zs[d]
        k = remote(gb.at[:, zz, 1 - core], r1.at[zz], a_send.at[zz], a_recv.at[zz], (partner, lon))
        k.start()
        first.append(k)
    sent = []
    for d, k in zip(order, first):
        zz = zs[d]
        k.wait_recv()
        total = gb[:, zz, core].astype(F32) + r1[zz].astype(F32)
        if d:
            sbuf[d] = total.astype(BF16)
            m = remote(sbuf.at[d], r2.at[z], z_send.at[d], z_recv.at[z], (lat_of(zz), lon))
            m.start()
            sent.append(m)
        else:
            acc[...] = total
    for d in (1, 7, 2, 6, 3, 5, 4):
        zz = zs[d]
        remote(sbuf.at[d], r2.at[zz], z_send.at[d], z_recv.at[zz], (lat_of(zz), lon)).wait_recv()
        acc[...] += r2[zz].astype(F32)
    own3[...] = acc[1 - yh].astype(BF16)
    y = remote(own3, r3, y_sem.at[0], y_sem.at[1], (across, lon))
    y.start()
    y.wait_recv()
    blk[...] = acc[yh] + r3[...].astype(F32)
    for shard, lane, row, at, length in group_map():
        pbuf[shard, :, lane : lane + length] = blk[row : row + 1, at : at + length]
    out = []
    for d in range(1, LON):
        p = lons[d - 1]
        k = remote(pbuf.at[p], r4.at[lon], l_send.at[d], l_recv.at[lon], (lat, p))
        k.start()
        out.append(k)
    r4[lon] = pbuf[lon]
    for d in range(1, LON):
        p = lons[d - 1]
        remote(pbuf.at[p], r4.at[p], l_send.at[d], l_recv.at[p], (lat, p)).wait_recv()
    total = r4[0]
    for n in range(1, LON):
        total = total + r4[n]
    total = total * (1.0 / LOSS_CELLS)
    o1[...] = total[:, 0:S1]
    o2[...] = total[:, S1 : S1 + S2]
    o3[...] = total[:, S1 + S2 :]
    for k in first + sent + [y] + out:
        k.wait_send()


def reduce_grads(gb):
    vm = pl.BlockSpec(memory_space=pltpu.VMEM)
    sds = jax.ShapeDtypeStruct
    V, D = pltpu.VMEM, pltpu.SemaphoreType.DMA
    return pl.pallas_call(
        reduce_kernel,
        out_shape=(sds((1, S1), F32), sds((1, S2), F32), sds((1, S2), F32)),
        in_specs=[vm],
        out_specs=(vm, vm, vm),
        scratch_shapes=[
            V((ZS, 2, 72, 384), BF16), V((ZS, 2, 72, 384), BF16), V((ZS, 2, 72, 384), BF16), V((2, 72, 384), F32),
            V((72, 384), BF16), V((72, 384), BF16), V((72, 384), F32), V((LON, 1, 3456), F32), V((LON, 1, 3456), F32),
            D((ZS,)), D((ZS,)), D((ZS,)), D((ZS,)), D((2,)), D((LON,)), D((LON,)),
        ],
        compiler_params=pltpu.CompilerParams(collective_id=1, has_side_effects=True),
        name="reduce_grads",
    )(gb)


def local(inputs, w_first, w_second, w_third, cotangent):
    v = jnp.concatenate([w_first, w_second, w_third]).astype(F32).reshape(1, -1)
    xe, xw, xn, xs, ce, cw, cn, cs, wb = gather(v, inputs, cotangent)
    where = jnp.stack([lax.axis_index("lat"), jnp.int32(lax.axis_size("lat") - 1)]).astype(jnp.int32)
    features, grad_input, gb = compute(where, inputs, xe, xw, xn, xs, cotangent, ce, cw, cn, cs, wb)
    g1, g2, g3 = reduce_grads(gb.reshape(2, ZS, 2, 72, 384))
    return features, grad_input, g1.reshape(-1), g2.reshape(-1), g3.reshape(-1)


def solution(mesh):
    tile, flat = P("lat", "lon", None), P(("lat", "lon"))
    return jax.shard_map(
        local,
        mesh=mesh,
        in_specs=(tile, flat, flat, flat, tile),
        out_specs=(tile, tile, flat, flat, flat),
        check_vma=False,
    )
```

time: 690 us -> 129 us (0.19); the launches traced: 681 us -> 128 us
  waiting for transfers between devices: 457 us -> 0 us
  local copies, waits for them, and re-layouts: 138 us -> 2.19 us
  Pallas kernels: 0 us -> 120 us
  starting transfers between devices: 38.9 us -> 0 us
  matrix products: 23.6 us -> 0 us
  between operations: 15.3 us -> 0.66 us
    unnamed x4 -> x0, waiting for transfers between devices: 448 us -> none
    pallas_call x0 -> x3, Pallas kernels: none -> 120 us  [the longest x1 54.9 us: gather(): pl.pallas_call(gather_kernel, out_shape=(sds((64, 16, 128), BF16), sds((6...]
    slice x17 -> x0, local copies, waits for them, and re-layouts: 84.6 us -> none  [the longest x11 83.4 us: kernel_grad(): padded[row_tap:row_tap + stride * (row_count - 1) + 1:stride, col_tap:col...]
    ppermute x20 -> x0, starting transfers between devices: 38.8 us -> none  [the longest x8 16.8 us: padded_2(): lax.ppermute(lax.slice_in_dim(block, block.shape[dim] - width, None, axis...]
    unnamed x76 -> x0, local copies, waits for them, and re-layouts: 19.5 us -> none
    dot_general x12 -> x0, matrix products: 16.3 us -> none  [the longest x3 9.63 us: kernel_grad(): lax.dot_general(columns, flat_deltas, (((0,), (0,)), ((), ())), preferred...]
    concatenate x3 -> x4, local copies, waits for them, and re-layouts: 14.5 us -> 2.19 us  [local(): v = jnp.concatenate([w_first, w_second, w_third]).astype(F32).reshape(1, -1)]
    mul x6 -> x0, local copies, waits for them, and re-layouts: 10.7 us -> none  [kernel_grad(): return product.reshape(-1) * factor]
  transfers between devices with their start and end apart: 22 -> 0, of which waited for: 8 -> 0; matrix products, arithmetic and copies ran while one was open for 20% -> 0% of each run, Pallas kernels for 0% -> 0%
where the time goes in v1:
time: 129 us; the launch traced here: 128 us
  Pallas kernels  120 us (93%)
  other arithmetic  5.11 us (4%)
  local copies, waits for them, and re-layouts  2.19 us (2%)
    pallas_call x1, Pallas kernels, gather(): pl.pallas_call(gather_kernel, out_shape=(sds((64, 16, 128), BF16), sds((6...  54.9 us
    pallas_call x1, Pallas kernels, reduce_grads(): pl.pallas_call(reduce_kernel, out_shape=(sds((1, S1), F32), sds((1, S2),...  38.1 us
    pallas_call x1, Pallas kernels, compute(): pl.pallas_call(compute_kernel, out_shape=(jax.ShapeDtypeStruct((32, 32, 1...  26.8 us
    pallas_call x3, other arithmetic, reduce_grads(): pl.pallas_call(reduce_kernel, out_shape=(sds((1, S1), F32), sds((1, S2),...  3.9 us

profile of v1, /device:TPU:2, one launch (start us, length us, event | category | flops | bytes accessed | tf_op | source)
XLA Modules:
  0.0 127.7 jit_solution(428689198765734831)
XLA Ops:
  0.6 0.6 pad_add_fusion.lat_ref
  1.2 0.7 concatenate.16
  1.9 0.7 concatenate.17
  2.6 0.7 concatenate.18
  3.3 0.1 concatenate.19
  3.4 0.6 convert_element_type.10.v_ref
  4.0 54.9 %gather_weights.1 = (bf16[64,16,128]{2,1,0:T(8,128)(2,1)}, bf16[64,16,128]{2,1,0:T(8,128)(2,1)}, bf16[10,96,128]{2,1,0:T(8,128)(2,1)}, bf16[10,96,128]{2,1,0:T(8...) custom-call(f32[1,3456]{1,0:T(1,128)} %convert_element_type.10.v_ref, ...), custom_call_target="tpu_custom_call" | custom-call | tf_op jit(solution)/shard_map/gather_weights/pallas_call | solution.py:385
  58.9 26.8 %level_compute.1 = (bf16[32,32,192]{2,1,0:T(8,128)(2,1)}, bf16[64,64,128]{2,1,0:T(8,128)(2,1)}, bf16[32,72,384]{2,1,0:T(8,128)(2,1)}) custom-call(s32[2]{0:T(128)} %pad_add_fusion.lat_ref, bf16[64,64,128]{2,1,0:T(8,128)(2,1)} %x_ref.3, bf16[64,16,128]{2,1,0:T(8,128)(2,1)} %get-tuple-element.20.xe_ref, bf16[64,16,128]{2,1,0:T(8,128)(2,1)} %get-tuple-element.21.xw_ref, ...), custom_call_target="tpu_custom_call" | custom-call | flops 8000000000 | bytes 8000000 | tf_op jit(solution)/shard_map/level_compute/pallas_call | solution.py:208
  85.7 38.1 %reduce_grads.1 = (f32[1,864]{1,0:T(1,128)}, f32[1,1296]{1,0:T(1,128)}, f32[1,1296]{1,0:T(1,128)}) custom-call(bf16[2,8,2,72,384]{4,3,2,1,0:T(8,128)(2,1)} %bitcast.2), custom_call_target="tpu_custom_call" | custom-call | tf_op jit(solution)/shard_map/reduce_grads/pallas_call | solution.py:472
  123.8 1.3 %reduce = f32[864]{0:T(1024)} reduce(f32[1,864]{1,0:T(1,128)} %get-tuple-element.32, f32[]{:T(128)} %constant.11), dimensions={0}, to_apply=%get-tuple-element.32.reduce_sub_computation | reduce | bytes 6916 | tf_op jit(solution)/shard_map/reduce_grads/pallas_call | solution.py:472
  125.1 1.3 %reduce.1 = f32[1296]{0:T(1024)} reduce(f32[1,1296]{1,0:T(1,128)} %get-tuple-element.33, f32[]{:T(128)} %constant.11), dimensions={0}, to_apply=%get-tuple-element.33.reduce_sub_computation | reduce | bytes 10372 | tf_op jit(solution)/shard_map/reduce_grads/pallas_call | solution.py:472
  126.4 1.3 %reduce.2 = f32[1296]{0:T(1024)} reduce(f32[1,1296]{1,0:T(1,128)} %get-tuple-element.34, f32[]{:T(128)} %constant.11), dimensions={0}, to_apply=%get-tuple-element.34.reduce_sub_computation | reduce | bytes 10372 | tf_op jit(solution)/shard_map/reduce_grads/pallas_call | solution.py:472

commit v2 on v0

v2 whole, which is shorter than its diff:
```python
import jax
import jax.numpy as jnp
from jax import lax
from jax.experimental import pallas as pl
from jax.experimental.pallas import tpu as pltpu
from jax.sharding import PartitionSpec as P

LOSS_CELLS = 1024
F32, BF16 = jnp.float32, jnp.bfloat16
W = 48
PITCH = 104
MESH = pl.DeviceIdType.MESH
LON, ZS, GROUPS = 8, 8, 32
S1, S2 = 864, 1296


def mm(a, b):
    return lax.dot_general(a, b, (((1,), (0,)), ((), ())), preferred_element_type=F32)


def mmt(a, b):
    return lax.dot_general(a, b, (((1,), (1,)), ((), ())), preferred_element_type=F32)


def pieces(size, fold):
    out = []
    for row in range(size * LON // 192):
        at = row * 192
        while at < (row + 1) * 192:
            shard = at // size
            end = min((row + 1) * 192, (shard + 1) * size)
            out.append((shard, at - shard * size, row % fold, 192 * (row // fold) + at - row * 192, end - at))
            at = end
    return out


def group_map():
    moves = [(s, lane, 54 + row, at, n) for s, lane, row, at, n in pieces(S1, 18)]
    for k in range(2):
        moves += [(s, S1 + k * S2 + lane, row, 192 * k + at, n) for s, lane, row, at, n in pieces(S2, 54)]
    return moves


def place():
    lat, lon = lax.axis_index("lat"), lax.axis_index("lon")
    core = lax.rem(lat, 2)
    z = lax.rem(lax.div(lat, 2), ZS)
    yh = lax.div(lat, 2 * ZS)
    return lat, lon, yh, z, core


def barrier(peers):
    sem = pltpu.get_barrier_semaphore()
    for peer in peers:
        pl.semaphore_signal(sem, inc=1, device_id=peer, device_id_type=MESH)
    pl.semaphore_wait(sem, len(peers))


def remote(src, dst, send, recv, peer):
    return pltpu.make_async_remote_copy(src_ref=src, dst_ref=dst, send_sem=send, recv_sem=recv,
                                        device_id=peer, device_id_type=MESH)


def gather_kernel(w1, w2, w3, x_ref, c_ref,
                  xe, xw, xn, xs, xne, xnw, xse, xsw, ce, cw, cn, cs, cne, cnw, cse, csw, wb,
                  v_ref, vbuf, stage, own, xin, col, eb, vsend, vrecv, hsend, hrecv, wsend, wrecv, osem, isem):
    lat, lon, yh, z, core = place()
    east, west = lax.rem(lon + 1, LON), lax.rem(lon + LON - 1, LON)
    north, south = lax.rem(lat + 31, 32), lax.rem(lat + 1, 32)
    partner = lat + 1 - 2 * core
    across = lax.rem(lat + 16, 32)
    def at_z(k):
        return yh * 16 + lax.rem(z + k + ZS, ZS) * 2 + core
    lons = [lax.rem(lon + d, LON) for d in range(1, LON)]

    edges = [pltpu.make_async_copy(x_ref.at[:, 16 * (3 * k) : 16 * (3 * k) + 16], xin.at[k], isem.at[k]) for k in range(2)]
    for k in edges:
        k.start()
    v_ref[0:1, 0:S1] = w1[...].astype(F32).reshape(1, S1)
    v_ref[0:1, S1 : S1 + S2] = w2[...].astype(F32).reshape(1, S2)
    v_ref[0:1, S1 + S2 :] = w3[...].astype(F32).reshape(1, S2)
    barrier([(lat, p) for p in lons] + [(q, lon) for q in (north, south, across, at_z(1), at_z(-1))])

    vs = []
    for d in range(1, LON):
        k = remote(v_ref, vbuf.at[lon], vsend.at[d], vrecv.at[lon], (lat, lons[d - 1]))
        k.start()
        vs.append(k)
    halos = []
    def halo(src, dst, peer):
        n = len(halos)
        k = remote(src, dst, hsend.at[n], hrecv.at[n], peer)
        k.start()
        halos.append(k)
    e, w, n, s = (lat, east), (lat, west), (north, lon), (south, lon)
    for k in range(2):
        edges[k].wait()
        col[...] = xin[k].astype(F32).reshape(1024, 128)
        for j in range(10):
            eb[k, j] = col[pl.ds(j + 6 * k, 64, stride=16), :].astype(BF16)
    halo(eb.at[0], xe, w)
    halo(eb.at[1], xw, e)
    halo(x_ref.at[54:64], xn, s)
    halo(x_ref.at[0:10], xs, n)

    vbuf[lon] = v_ref[...]
    for d in range(1, LON):
        src = lons[d - 1]
        remote(v_ref, vbuf.at[src], vsend.at[d], vrecv.at[src], (lat, src)).wait_recv()
    for shard, lane, row, at, length in group_map():
        stage[row : row + 1, at : at + length] = vbuf[shard, :, lane : lane + length]
    own[...] = stage[...].astype(BF16)

    started = []
    def send(src, slot, peer):
        k = remote(src, wb.at[slot], wsend.at[len(started)], wrecv.at[slot], peer)
        k.start()
        started.append(k)
    def arrived(slot):
        remote(own, wb.at[slot], wsend.at[0], wrecv.at[slot], (partner, lon)).wait_recv()
    up, down = (at_z(1), lon), (at_z(-1), lon)
    mine = pltpu.make_async_copy(own, wb.at[lat], osem)
    mine.start()
    send(own, lat, (across, lon))
    send(own, lat, up)
    send(own, lat, down)
    send(own, lat, (partner, lon))
    halo(c_ref.at[:, 0:8], ce, w)
    halo(c_ref.at[:, 24:32], cw, e)
    halo(c_ref.at[29:32], cn, s)
    halo(c_ref.at[0:3], cs, n)

    def slot_of(half, k):
        return half * 16 + lax.rem(z + k + ZS, ZS) * 2 + core
    other = 1 - yh
    second = slot_of(other, 0)
    def pass_on(half, t, sign, last):
        slot = slot_of(half, -sign * t)
        arrived(slot)
        if t < last:
            send(wb.at[slot], slot, up if sign > 0 else down)
        send(wb.at[slot], slot, (partner, lon))
    for t in range(0, 5):
        if t >= 1:
            if t <= 4:
                pass_on(yh, t, 1, 4)
            if t <= 3:
                pass_on(yh, t, -1, 3)
        if t == 0:
            arrived(second)
            send(wb.at[second], second, up)
            send(wb.at[second], second, down)
            send(wb.at[second], second, (partner, lon))
        else:
            if t <= 3:
                pass_on(other, t, 1, 3)
            if t <= 4:
                pass_on(other, t, -1, 4)
        if t == 2:
            halos[0].wait_recv()
            halos[1].wait_recv()
            halo(xe.at[:, 48:64], xne, s)
            halo(xw.at[:, 48:64], xnw, s)
            halo(xe.at[:, 0:16], xse, n)
            halo(xw.at[:, 0:16], xsw, n)
        if t == 3:
            halos[4].wait_recv()
            halos[5].wait_recv()
            halo(ce.at[29:32], cne, s)
            halo(cw.at[29:32], cnw, s)
            halo(ce.at[0:3], cse, n)
            halo(cw.at[0:3], csw, n)
    for half in range(2):
        for k in range(ZS):
            arrived(half * 16 + k * 2 + 1 - core)
    mine.wait()
    for k in started:
        k.wait_send()
    for k in vs:
        k.wait_send()
    for n, k in enumerate(halos):
        k.wait_send()
        if n not in (0, 1, 4, 5):
            k.wait_recv()


def gather(w1, w2, w3, x, c):
    anyspec = pl.BlockSpec(memory_space=pl.ANY)
    vm = pl.BlockSpec(memory_space=pltpu.VMEM)
    shapes = ([(10, 64, 128)] * 4 + [(10, 16, 128)] * 4 + [(32, 8, 192)] * 2 + [(3, 32, 192)] * 2 + [(3, 8, 192)] * 4
              + [(32, 72, 384)])
    D = pltpu.SemaphoreType.DMA
    return pl.pallas_call(
        gather_kernel,
        out_shape=tuple(jax.ShapeDtypeStruct(s, BF16) for s in shapes),
        in_specs=[vm, vm, vm, anyspec, anyspec],
        out_specs=(anyspec,) * len(shapes),
        scratch_shapes=[
            pltpu.VMEM((1, 3456), F32), pltpu.VMEM((LON, 1, 3456), F32), pltpu.VMEM((72, 384), F32),
            pltpu.VMEM((72, 384), BF16), pltpu.VMEM((2, 64, 16, 128), BF16), pltpu.VMEM((1024, 128), F32),
            pltpu.VMEM((2, 10, 64, 128), BF16),
            D((LON,)), D((LON,)), D((16,)), D((16,)), D((34,)), D((GROUPS,)), D, D((2,)),
        ],
        compiler_params=pltpu.CompilerParams(collective_id=0, has_side_effects=True),
        name="gather_weights",
    )(w1, w2, w3, x, c)


def level_kernel(x_ref, xe, xw, xn, xs, xne, xnw, xse, xsw, c_ref, ce, cw, cn, cs, cne, cnw, cse, csw, w_ref,
                 feat_ref, gin_ref, o1, o2, o3,
                 xf, x0, x1, kf, kg, k1, k2, k3, cf, hs1, hs2, ds3, ds2, bs, p2, dt, g1, g2, g3, st, il,
                 a3, a2, a1, r3, r2, r1, s3, s2, s1, z3, z2, z1, acc3, acc2, acc1, y3s, y2s, y1s, y3, y2, y1,
                 blk, p23, p1, l23, l1, a_send, a_recv, z_send, z_recv, y_send, y_recv, l_send, l_recv):
    lat, lon, yh, z, core = place()
    last = lax.axis_size("lat") - 1
    partner = lat + 1 - 2 * core
    across = lax.rem(lat + 16, 32)
    lons = [lax.rem(lon + d, LON) for d in range(1, LON)]
    zs = [lax.rem(z + d, ZS) for d in range(ZS)]
    def lat_of(zz):
        return yh * 16 + zz * 2 + core
    barrier([(lat, p) for p in lons] + [(partner, lon), (across, lon)] + [(lat_of(zz), lon) for zz in zs[1:]])

    for g in range(32):
        v = w_ref[g].astype(F32)
        kf[54 * g : 54 * g + 54, :] = v[0:54]
        kg[36 * g : 36 * g + 18, :] = v[54:72, 0:192]
        kg[36 * g + 18 : 36 * g + 36, :] = v[54:72, 192:384]
    k1[...] = kg[...].astype(BF16)
    k2[...] = kf[:, 0:192].astype(BF16)
    k3[...] = kf[:, 192:384].astype(BF16)
    north = (lat > 0).astype(F32)
    south = (lat < last).astype(F32)

    def own_row(r, _):
        p = pl.multiple_of((r + 9) * PITCH, 8)
        xf[pl.ds(p + 8, 64), :] = x_ref[r].astype(F32)
        xf[pl.ds(p + 80, 16), :] = jnp.zeros((16, 128), F32)
        return 0
    lax.fori_loop(0, 64, own_row, 0)
    for q in range(9):
        xf[q * PITCH + 8 : q * PITCH + 72, :] = xn[q + 1].astype(F32) * north
        xf[q * PITCH + 80 : q * PITCH + 96, :] = jnp.zeros((16, 128), F32)
    for q in range(10):
        xf[(q + 73) * PITCH + 8 : (q + 73) * PITCH + 72, :] = xs[q].astype(F32) * south
        xf[(q + 73) * PITCH + 80 : (q + 73) * PITCH + 96, :] = jnp.zeros((16, 128), F32)
    for j in range(10):
        for ref, rn, rs, ats in ((xe, xne, xse, (72 + j,)), (xw, xnw, xsw, (94 + j, j - 2))):
            mid = ref[j].astype(F32)
            top = rn[j].astype(F32)[7:16] * north
            low = rs[j].astype(F32)[0:10] * south
            for at in ats:
                if at >= 0:
                    xf[pl.ds(9 * PITCH + at, 64, stride=PITCH), :] = mid
                    xf[pl.ds(at, 9, stride=PITCH), :] = top
                    xf[pl.ds(73 * PITCH + at, 10, stride=PITCH), :] = low
    def split(dst, p, idx):
        for k in range(3):
            dst[idx, :, 128 * k : 128 * k + 128] = xf[pl.ds(p * PITCH + 7 + k, W, stride=2), :].astype(BF16)
    def split_pair(k, _):
        split(x0, 2 * k, k)
        split(x1, 2 * k + 1, k)
        return 0
    lax.fori_loop(0, 41, split_pair, 0)
    split(x0, 82, 41)

    def cot(idx, row, e, w):
        cf[idx, 0:32, :] = row.astype(F32)
        cf[idx, 32:40, :] = e.astype(F32)
        cf[idx, 40:48, :] = w.astype(F32)
    def cot_own(k, _):
        cot(k + 2, c_ref[k], ce[k], cw[k])
        return 0
    lax.fori_loop(0, 32, cot_own, 0)
    for q in range(2):
        cot(q, cn[q + 1], cne[q + 1], cnw[q + 1])
    for q in range(3):
        cot(q + 34, cs[q], cse[q], csw[q])

    def rows_ok(start, n, first):
        i = lax.broadcasted_iota(jnp.int32, (n, W, 192), 0) + (start + first)
        glob = i + 32 * lat
        return (glob >= 0) & (glob < 32 * (last + 1))
    def put_shifted(dst, start, n, value):
        dst[1, pl.ds(start, n)] = value.astype(BF16)
        dst[0, pl.ds(start, n)] = pltpu.roll(value, 1, 1).astype(BF16)
        dst[2, pl.ds(start, n)] = pltpu.roll(value, W - 1, 1).astype(BF16)
    def chunks(total, n, body, lo=0, hi=None):
        count = -(-total // n)
        def step(k, _):
            body(jnp.minimum(k * n, total - n))
            return 0
        lax.fori_loop(lo, count if hi is None else hi, step, 0)

    def h_one(s):
        n = 14
        acc = mm(x0[pl.ds(s, n)].reshape(n * W, 384), k1[0:384])
        acc += mm(x1[pl.ds(s, n)].reshape(n * W, 384), k1[384:768])
        acc += mm(x0[pl.ds(s + 1, n)].reshape(n * W, 384), k1[768:1152])
        put_shifted(hs1, s, n, jnp.where(rows_ok(s, n, -4), acc.reshape(n, W, 192), 0.0))
    chunks(41, 14, h_one)

    def conv(src, k, s, n):
        acc = None
        for a in range(3):
            for b in range(3):
                t = mm(src[b, pl.ds(s + a, n)].reshape(n * W, 192), k[(3 * a + b) * 192 : (3 * a + b + 1) * 192])
                acc = t if acc is None else acc + t
        return acc.reshape(n, W, 192)
    def tconv(src, k, s, n):
        acc = None
        for a in range(3):
            for b in range(3):
                t = mmt(src[2 - b, pl.ds(s + 2 - a, n)].reshape(n * W, 192), k[(3 * a + b) * 192 : (3 * a + b + 1) * 192])
                acc = t if acc is None else acc + t
        return acc.reshape(n, W, 192)

    def h_two(s):
        n = 13
        v = conv(hs1, k2, s, n)
        p2[pl.ds(s, n)] = v
        h = v / (1.0 + jnp.exp(-v))
        put_shifted(hs2, s, n, jnp.where(rows_ok(s, n, -3), h, 0.0))
    chunks(39, 13, h_two)

    def deriv(v):
        sg = 1.0 / (1.0 + jnp.exp(-v))
        return sg, sg * (1.0 + v * (1.0 - sg))
    def d_three(s):
        n = 13
        v = conv(hs2, k3, s, n)
        sg, dv = deriv(v)
        bs[1, pl.ds(s, n)] = (v * sg).astype(BF16)
        put_shifted(ds3, s, n, jnp.where(rows_ok(s, n, -2), cf[pl.ds(s, n)] * dv, 0.0))
    chunks(37, 13, d_three)
    feat_ref[...] = bs[1, 2:34, 0:32, :]

    def wgrad(src, off, dst):
        for a in range(3):
            for b in range(3):
                win = src[b, off + a : off + a + 32, 0:32, :].reshape(1024, 192)
                t = mm(dt[...], win)
                n0 = (3 * a + b) * 192
                dst[n0 : n0 + 192, :] = t.T
    sends = []
    def to_partner(i, g, half, a, r):
        for zz in range(ZS):
            for c in range(2):
                for y in range(2):
                    base = (y * 16 + zz * 2 + c) * 2 * half
                    st[y * half : (y + 1) * half, 0:192] = g[base : base + half, :]
                    st[y * half : (y + 1) * half, 192:384] = g[base + half : base + 2 * half, :]
                a[zz, c] = st[0 : 2 * half, :].astype(BF16)
        k = remote(a.at[:, 1 - core], r, a_send.at[i], a_recv.at[i], (partner, lon))
        k.start()
        sends.append(k)
        return k
    def along_z(i, k, a, r, s, zb, acc):
        k.wait_recv()
        for d in (4, 3, 5, 2, 6, 1, 7, 0):
            zz = zs[d]
            total = a[zz, core].astype(F32) + r[zz].astype(F32)
            if d:
                s[d] = total.astype(BF16)
                m = remote(s.at[d], zb.at[z], z_send.at[i, d], z_recv.at[i, z], (lat_of(zz), lon))
                m.start()
                sends.append(m)
            else:
                acc[...] = total
    def sum_z(i, s, zb, acc, half, ys, yr):
        for d in (1, 7, 2, 6, 3, 5, 4):
            zz = zs[d]
            remote(s.at[d], zb.at[zz], z_send.at[i, d], z_recv.at[i, zz], (lat_of(zz), lon)).wait_recv()
            acc[...] += zb[zz].astype(F32)
        ys[...] = jnp.where(yh == 0, acc[half : 2 * half], acc[0:half]).astype(BF16)
        m = remote(ys, yr, y_send.at[i], y_recv.at[i], (across, lon))
        m.start()
        sends.append(m)
        return m
    def sum_y(m, acc, half, yr):
        m.wait_recv()
        blk[0:half, :] = jnp.where(yh == 0, acc[0:half], acc[half : 2 * half]) + yr[...].astype(F32)
    def to_lon(i, pb, lb):
        for d in range(1, LON):
            p = lons[d - 1]
            k = remote(pb.at[p], lb.at[lon], l_send.at[i, d], l_recv.at[i, lon], (lat, p))
            k.start()
            sends.append(k)
        lb[lon] = pb[lon]
    def sum_lon(i, pb, lb):
        for d in range(1, LON):
            p = lons[d - 1]
            remote(pb.at[p], lb.at[p], l_send.at[i, d], l_recv.at[i, p], (lat, p)).wait_recv()
        total = lb[0]
        for n in range(1, LON):
            total = total + lb[n]
        return total * (1.0 / LOSS_CELLS)

    dt[...] = ds3[1, 2:34, 0:32, :].reshape(1024, 192).T
    wgrad(hs2, 2, g3)
    c3 = to_partner(0, g3, 27, a3, r3)

    def d_two(s):
        n = 12
        v = tconv(ds3, k3, s, n)
        _, dv = deriv(p2[pl.ds(s + 2, n)])
        put_shifted(ds2, s, n, jnp.where(rows_ok(s, n, -1), v * dv, 0.0))
    chunks(35, 12, d_two)
    along_z(0, c3, a3, r3, s3, z3, acc3)
    dt[...] = ds2[1, 1:33, 0:32, :].reshape(1024, 192).T
    wgrad(hs1, 3, g2)
    c2 = to_partner(1, g2, 27, a2, r2)

    def b_one(s):
        n = 11
        v = jnp.where(rows_ok(s, n, 0), tconv(ds2, k2, s, n), 0.0)
        bs[1, pl.ds(s, n)] = v.astype(BF16)
        bs[2, pl.ds(s, n)] = pltpu.roll(v, W - 1, 1).astype(BF16)
    chunks(33, 11, b_one)
    along_z(1, c2, a2, r2, s2, z2, acc2)
    dt[...] = bs[1, 0:32, 0:32, :].reshape(1024, 192).T
    for a in range(3):
        src = x1 if a == 1 else x0
        off = 4 + (a == 2)
        win = src[off : off + 32, 0:32, :].reshape(1024, 384)
        g1[384 * a : 384 * a + 384, :] = mm(dt[...], win).T
    c1 = to_partner(2, g1, 18, a1, r1)

    def k1t(a, b):
        n0 = (3 * a + b) * 128
        return k1[n0 : n0 + 128]
    def gin(i):
        n = 8
        here = bs[1, pl.ds(i, n), 0:32, :].reshape(n * 32, 192)
        right = bs[2, pl.ds(i, n), 0:32, :].reshape(n * 32, 192)
        below = bs[1, pl.ds(i + 1, n), 0:32, :].reshape(n * 32, 192)
        corner = bs[2, pl.ds(i + 1, n), 0:32, :].reshape(n * 32, 192)
        ee = mmt(here, k1t(1, 1))
        eo = mmt(right, k1t(1, 0)) + mmt(here, k1t(1, 2))
        oe = mmt(below, k1t(0, 1)) + mmt(here, k1t(2, 1))
        oo = mmt(corner, k1t(0, 0)) + mmt(below, k1t(0, 2)) + mmt(right, k1t(2, 0)) + mmt(here, k1t(2, 2))
        il[pl.ds(0, n * 32, stride=2), :] = ee
        il[pl.ds(1, n * 32, stride=2), :] = eo
        il[pl.ds(n * 64, n * 32, stride=2), :] = oe
        il[pl.ds(n * 64 + 1, n * 32, stride=2), :] = oo
        even = il[0 : n * 64, :].reshape(n, 64, 128).astype(BF16)
        odd = il[n * 64 : n * 128, :].reshape(n, 64, 128).astype(BF16)
        for m in range(n):
            gin_ref[2 * (i + m)] = even[m]
            gin_ref[2 * (i + m) + 1] = odd[m]
    chunks(32, 8, gin, 0, 1)
    along_z(2, c1, a1, r1, s1, z1, acc1)
    chunks(32, 8, gin, 1, 4)

    m3 = sum_z(0, s3, z3, acc3, 27, y3s, y3)
    m2 = sum_z(1, s2, z2, acc2, 27, y2s, y2)
    sum_y(m3, acc3, 27, y3)
    for shard, lane, row, at, length in pieces(S2, 27):
        p23[shard, :, S2 + lane : S2 + lane + length] = blk[row : row + 1, at : at + length]
    sum_y(m2, acc2, 27, y2)
    for shard, lane, row, at, length in pieces(S2, 27):
        p23[shard, :, lane : lane + length] = blk[row : row + 1, at : at + length]
    to_lon(0, p23, l23)
    m1 = sum_z(2, s1, z1, acc1, 18, y1s, y1)
    total = sum_lon(0, p23, l23)
    o2[...] = total[:, 0:S2].reshape(S2)
    o3[...] = total[:, S2:].reshape(S2)
    sum_y(m1, acc1, 18, y1)
    for shard, lane, row, at, length in pieces(S1, 18):
        p1[shard, :, lane : lane + length] = blk[row : row + 1, at : at + length]
    to_lon(1, p1, l1)
    o1[...] = sum_lon(1, p1, l1).reshape(S1)
    for k in sends:
        k.wait_send()


def level(x, c, halos):
    V, D = pltpu.VMEM, pltpu.SemaphoreType.DMA
    vm = pl.BlockSpec(memory_space=pltpu.VMEM)
    sds = jax.ShapeDtypeStruct
    args = (x, *halos[0:8], c, *halos[8:17])
    def over_rows(*shape_of):
        return [V(shape_of[0](rows), shape_of[1]) for rows in (54, 54, 36)]
    return pl.pallas_call(
        level_kernel,
        out_shape=(sds((32, 32, 192), BF16), sds((64, 64, 128), BF16), sds((S1,), F32), sds((S2,), F32), sds((S2,), F32)),
        in_specs=[vm] * len(args),
        out_specs=(vm,) * 5,
        scratch_shapes=[
            V((83 * PITCH, 128), F32), V((42, W, 384), BF16), V((42, W, 384), BF16),
            V((1728, 384), F32), V((1152, 192), F32), V((1152, 192), BF16), V((1728, 192), BF16), V((1728, 192), BF16),
            V((37, W, 192), F32), V((3, 41, W, 192), BF16), V((3, 39, W, 192), BF16),
            V((3, 37, W, 192), BF16), V((3, 35, W, 192), BF16), V((3, 37, W, 192), BF16),
            V((39, W, 192), F32), V((192, 1024), BF16), V((1152, 192), F32), V((1728, 192), F32), V((1728, 192), F32),
            V((54, 384), F32), V((1024, 128), F32),
            *over_rows(lambda r: (ZS, 2, r, 384), BF16),
            *over_rows(lambda r: (ZS, r, 384), BF16),
            *over_rows(lambda r: (ZS, r, 384), BF16),
            *over_rows(lambda r: (ZS, r, 384), BF16),
            *over_rows(lambda r: (r, 384), F32),
            *over_rows(lambda r: (r // 2, 384), BF16),
            *over_rows(lambda r: (r // 2, 384), BF16),
            V((27, 384), F32), V((LON, 1, 2 * S2), F32), V((LON, 1, S1), F32), V((LON, 1, 2 * S2), F32), V((LON, 1, S1), F32),
            D((3,)), D((3,)), D((3, ZS)), D((3, ZS)), D((3,)), D((3,)), D((2, LON)), D((2, LON)),
        ],
        compiler_params=pltpu.CompilerParams(collective_id=1, has_side_effects=True, vmem_limit_bytes=62 * 1024 * 1024),
        name="level",
    )(*args)


def local(inputs, w_first, w_second, w_third, cotangent):
    halos = gather(w_first, w_second, w_third, inputs, cotangent)
    return level(inputs, cotangent, halos)


def solution(mesh):
    tile, flat = P("lat", "lon", None), P(("lat", "lon"))
    return jax.shard_map(
        local,
        mesh=mesh,
        in_specs=(tile, flat, flat, flat, tile),
        out_specs=(tile, tile, flat, flat, flat),
        check_vma=False,
    )
```

time: 690 us -> 104 us (0.15); the launches traced: 681 us -> 104 us
  waiting for transfers between devices: 457 us -> 0 us
  local copies, waits for them, and re-layouts: 138 us -> 4.73 us
  Pallas kernels: 0 us -> 98.2 us
  starting transfers between devices: 38.9 us -> 0 us
  matrix products: 23.6 us -> 0 us
  between operations: 15.3 us -> 0.68 us
  other arithmetic: 8.46 us -> 0 us
    unnamed x4 -> x0, waiting for transfers between devices: 448 us -> none
    pallas_call x0 -> x2, Pallas kernels: none -> 98.2 us  [the longest x1 55.3 us: level(): pl.pallas_call(level_kernel, out_shape=(sds((32, 32, 192), BF16), sds((64...]
    slice x17 -> x0, local copies, waits for them, and re-layouts: 84.6 us -> none  [the longest x11 83.4 us: kernel_grad(): padded[row_tap:row_tap + stride * (row_count - 1) + 1:stride, col_tap:col...]
    ppermute x20 -> x0, starting transfers between devices: 38.8 us -> none  [the longest x8 16.8 us: padded_2(): lax.ppermute(lax.slice_in_dim(block, block.shape[dim] - width, None, axis...]
    dot_general x12 -> x0, matrix products: 16.3 us -> none  [the longest x3 9.63 us: kernel_grad(): lax.dot_general(columns, flat_deltas, (((0,), (0,)), ((), ())), preferred...]
    unnamed x76 -> x13, local copies, waits for them, and re-layouts: 19.5 us -> 4.73 us
    concatenate x3 -> x0, local copies, waits for them, and re-layouts: 14.5 us -> none  [kernel_grad(): jnp.concatenate(windows, axis=2).reshape(row_count * col_count, -1)]
    mul x6 -> x0, local copies, waits for them, and re-layouts: 10.7 us -> none  [kernel_grad(): return product.reshape(-1) * factor]
  transfers between devices with their start and end apart: 22 -> 0, of which waited for: 8 -> 0; matrix products, arithmetic and copies ran while one was open for 20% -> 0% of each run, Pallas kernels for 0% -> 0%
where the time goes in v2:
time: 104 us
  Pallas kernels  98.2 us (94%)
  local copies, waits for them, and re-layouts  4.73 us (5%)
    pallas_call x1, Pallas kernels, level(): pl.pallas_call(level_kernel, out_shape=(sds((32, 32, 192), BF16), sds((64...  55.3 us
    pallas_call x1, Pallas kernels, gather(): pl.pallas_call(gather_kernel, out_shape=tuple((jax.ShapeDtypeStruct(s, BF...  42.9 us
    unnamed x13, local copies, waits for them, and re-layouts  4.73 us

profile of v2, /device:TPU:2, one launch (start us, length us, event | category | flops | bytes accessed | tf_op | source)
XLA Modules:
  0.0 103.6 jit_solution(12981214922338296410)
XLA Ops:
  0.6 42.9 %gather_weights.1 = (bf16[10,64,128]{2,1,0:T(8,128)(2,1)}, bf16[10,64,128]{2,1,0:T(8,128)(2,1)}, bf16[10,64,128]{2,1,0:T(8,128)(2,1)}, bf16[10,64,128]{2,1,0:T(8...) custom-call(bf16[864]{0:T(1024)(128)(2,1)} %w1.1, ...), custom_call_target="tpu_custom_call" | custom-call | tf_op jit(solution)/shard_map/gather_weights/pallas_call | solution.py:193
  43.5 55.3 %level.1 = (bf16[32,32,192]{2,1,0:T(8,128)(2,1)}, bf16[64,64,128]{2,1,0:T(8,128)(2,1)}, f32[864]{0:T(1024)}, f32[1296]{0:T(1024)}, f32[1296]{0:T(1024)}) custom-call(bf16[64,64,128]{2,1,0:T(8,128)(2,1)} %x_ref.3, bf16[10,64,128]{2,1,0:T(8,128)(2,1)} %get-tuple-element.22.xe, bf16[10,64,128]{2,1,0:T(8,128)(2,1)} %get-tuple-element.23.xw, ...), custom_call_target="tpu_custom_call" | custom-call | tf_op jit(solution)/shard_map/level/pallas_call | solution.py:484
  98.8 0.0 copy-start
  98.8 0.0 copy-start.3
  98.8 0.0 copy-start.2
  98.9 0.0 copy-start.1
  98.9 2.0 %copy.15 = bf16[32,32,192]{2,1,0:T(8,128)(2,1)} copy(bf16[32,32,192]{2,1,0:T(8,128)(2,1)} %get-tuple-element.44) | data formatting | bytes 786432
  100.8 0.0 copy-done
  100.8 1.0 copy.16
  101.8 0.0 copy-done.3
  101.8 0.6 copy.17
  102.4 0.0 copy-done.2
  102.4 0.6 copy.18
  103.0 0.0 copy-done.1
  103.0 0.6 copy.19
Async XLA Ops:
  98.8 2.0 %copy-start = (bf16[64,64,128]{2,1,0:T(8,128)(2,1)S(1)}, bf16[64,64,128]{2,1,0:T(8,128)(2,1)}, u32[]{:S(2)}) copy-start(bf16[64,64,128]{2,1,0:T(8,128)(2,1)} %get-tuple-element.45) | copy-start | bytes 3145732
  98.8 3.0 %copy-start.3 = (f32[864]{0:T(1024)S(1)}, f32[864]{0:T(1024)}, u32[]{:S(2)}) copy-start(f32[864]{0:T(1024)} %get-tuple-element.46) | copy-start | bytes 10372
  98.8 3.5 %copy-start.2 = (f32[1296]{0:T(1024)S(1)}, f32[1296]{0:T(1024)}, u32[]{:S(2)}) copy-start(f32[1296]{0:T(1024)} %get-tuple-element.47) | copy-start | bytes 15556
  98.9 4.1 %copy-start.1 = (f32[1296]{0:T(1024)S(1)}, f32[1296]{0:T(1024)}, u32[]{:S(2)}) copy-start(f32[1296]{0:T(1024)} %get-tuple-element.48) | copy-start | bytes 15556

commit v3 on v2

v3 whole, which is shorter than its diff:
```python
import jax
import jax.numpy as jnp
from jax import lax
from jax.experimental import pallas as pl
from jax.experimental.pallas import tpu as pltpu
from jax.sharding import PartitionSpec as P

LOSS_CELLS = 1024
F32, BF16 = jnp.float32, jnp.bfloat16
W = 48
PITCH = 104
MESH = pl.DeviceIdType.MESH
LON, ZS, GROUPS = 8, 8, 32
S1, S2 = 864, 1296
XS = 4
ROWS = (14, 14, 9)
STARTS = ((0, 13, 27, 40), (0, 13, 27, 40), (0, 9, 18, 27))


def mm(a, b):
    return lax.dot_general(a, b, (((1,), (0,)), ((), ())), preferred_element_type=F32)


def mmt(a, b):
    return lax.dot_general(a, b, (((1,), (1,)), ((), ())), preferred_element_type=F32)


def pieces(size, fold):
    out = []
    for row in range(size * LON // 192):
        at = row * 192
        while at < (row + 1) * 192:
            shard = at // size
            end = min((row + 1) * 192, (shard + 1) * size)
            out.append((shard, at - shard * size, row % fold, 192 * (row // fold) + at - row * 192, end - at))
            at = end
    return out


def group_map():
    moves = [(s, lane, 54 + row, at, n) for s, lane, row, at, n in pieces(S1, 18)]
    for k in range(2):
        moves += [(s, S1 + k * S2 + lane, row, 192 * k + at, n) for s, lane, row, at, n in pieces(S2, 54)]
    return moves


def flat_moves(size, shift):
    out = []
    for piece in range(2):
        lane = 0
        while lane < size:
            at = shift + piece * size + lane
            n = min(size - lane, 192 - at % 192)
            out.append((piece, lane, at // 192, at % 192, n))
            lane += n
    return out


def place():
    lat, lon = lax.axis_index("lat"), lax.axis_index("lon")
    core = lax.rem(lat, 2)
    z = lax.rem(lax.div(lat, 2), ZS)
    yh = lax.div(lat, 2 * ZS)
    x = lax.div(lon, 2)
    yl = lax.rem(lon, 2)
    return lat, lon, yh, z, core, x, yl


def remote(src, dst, send, recv, peer):
    return pltpu.make_async_remote_copy(src_ref=src, dst_ref=dst, send_sem=send, recv_sem=recv,
                                        device_id=peer, device_id_type=MESH)


def level_kernel(w1, w2, w3, x_hbm, c_hbm, feat_ref, gin_ref, o1, o2, o3,
                 x_ref, c_ref, v_ref, vbuf, stage, own, eb, xe, xw, xn, xs, xne, xnw, xse, xsw,
                 ce, cw, cn, cs, cne, cnw, cse, csw, wb, tr,
                 xf, x0, x1, kf2, kf3, kg, k1, k2, k3, cf, hs1, hs2, ds3, ds2, bs, p2, dt, g1, g2, g3, st, il,
                 a3, a2, a1, r3, r2, r1, s3, s2, s1, q3, q2, q1, acc3, acc2, acc1, t3, t2, t1, z3, z2, z1,
                 u3, u2, u1, f3, f2, f1, l3, l2, l1,
                 isem, vsend, vrecv, hsend, hrecv, wsend, wrecv, fsend, psend, precv,
                 a_send, a_recv, x_send, x_recv, z_send, z_recv, y_send, y_recv):
    lat, lon, yh, z, core, x, yl = place()
    last = lax.axis_size("lat") - 1
    east, west = lax.rem(lon + 1, LON), lax.rem(lon + LON - 1, LON)
    north_of, south_of = lax.rem(lat + 31, 32), lax.rem(lat + 1, 32)
    partner = lat + 1 - 2 * core
    across = lax.rem(lat + 16, 32)
    beside = lon + 1 - 2 * yl
    lons = [lax.rem(lon + d, LON) for d in range(1, LON)]
    xq = [lax.rem(x + d, XS) for d in range(XS)]
    zs = [lax.rem(z + d, ZS) for d in range(ZS)]
    def lat_of(half, zz):
        return half * 16 + zz * 2 + core
    near = (1, 7, 2, 6, 3, 5, 4)
    lats = [lat_of(yh, zs[d]) for d in near] + [lat_of(1 - yh, zs[d]) for d in (0, *near)]

    ins = [pltpu.make_async_copy(x_hbm, x_ref, isem.at[0]), pltpu.make_async_copy(c_hbm, c_ref, isem.at[1])]
    for k in ins:
        k.start()
    v_ref[0:1, 0:S1] = w1[...].astype(F32).reshape(1, S1)
    v_ref[0:1, S1 : S1 + S2] = w2[...].astype(F32).reshape(1, S2)
    v_ref[0:1, S1 + S2 :] = w3[...].astype(F32).reshape(1, S2)
    sem = pltpu.get_barrier_semaphore()
    peers = [(lat, p) for p in lons] + [(q, lon) for q in (north_of, south_of, *lats)] + [(across, beside)]
    for peer in peers:
        pl.semaphore_signal(sem, inc=1, device_id=peer, device_id_type=MESH)
    pl.semaphore_wait(sem, len(peers))

    sends = []
    for d in range(1, LON):
        k = remote(v_ref, vbuf.at[lon], vsend.at[d], vrecv.at[lon], (lat, lons[d - 1]))
        k.start()
        sends.append(k)
    halos = []
    def halo(src, dst, peer):
        n = len(halos)
        k = remote(src, dst, hsend.at[n], hrecv.at[n], peer)
        k.start()
        halos.append(k)
        sends.append(k)
    e, w, n, s = (lat, east), (lat, west), (north_of, lon), (south_of, lon)
    halo(x_hbm.at[54:64], xn, s)
    halo(x_hbm.at[0:10], xs, n)
    ins[0].wait()
    for k in range(2):
        il[...] = x_ref[:, 48 * k : 48 * k + 16, :].astype(F32).reshape(1024, 128)
        for j in range(10):
            eb[k, j] = il[pl.ds(j + 6 * k, 64, stride=16), :].astype(BF16)
    halo(eb.at[0], xe, w)
    halo(eb.at[1], xw, e)
    ins[1].wait()

    vbuf[lon] = v_ref[...]
    for d in range(1, LON):
        src = lons[d - 1]
        remote(v_ref, vbuf.at[src], vsend.at[d], vrecv.at[src], (lat, src)).wait_recv()
    for shard, lane, row, at, length in group_map():
        stage[row : row + 1, at : at + length] = vbuf[shard, :, lane : lane + length]
    for t in range(3):
        tr[72 * t : 72 * t + 72, :] = stage[:, 128 * t : 128 * t + 128]
    tr[216:224, :] = jnp.zeros((8, 128), F32)
    for k in range(XS):
        own[k] = tr[56 * k : 56 * k + 56, :].astype(BF16)
    for i, q in enumerate(lats):
        k = remote(own.at[x], wb.at[lat, x], wsend.at[i], wrecv.at[lat, x], (q, lon))
        k.start()
        sends.append(k)
    k = remote(own, wb.at[lat], psend.at[15], precv.at[lat], (partner, lon))
    k.start()
    sends.append(k)
    wb[lat] = own[...]

    north = (lat > 0).astype(F32)
    south = (lat < last).astype(F32)
    def own_row(r, _):
        p = pl.multiple_of((r + 9) * PITCH, 8)
        xf[pl.ds(p + 8, 64), :] = x_ref[r].astype(F32)
        xf[pl.ds(p + 80, 16), :] = jnp.zeros((16, 128), F32)
        return 0
    lax.fori_loop(0, 64, own_row, 0)
    def forward(i):
        q = lats[i]
        remote(own.at[x], wb.at[q, x], wsend.at[i], wrecv.at[q, x], (q, lon)).wait_recv()
        for d in range(1, XS):
            k = remote(wb.at[q, x], wb.at[q, x], fsend.at[i, d], wrecv.at[q, x], (lat, xq[d] * 2 + yl))
            k.start()
            sends.append(k)
    def share(i):
        q = lats[i]
        for d in range(1, XS):
            remote(own.at[x], wb.at[q, xq[d]], fsend.at[i, d], wrecv.at[q, xq[d]], (lat, xq[d] * 2 + yl)).wait_recv()
        k = remote(wb.at[q], wb.at[q], psend.at[i], precv.at[q], (partner, lon))
        k.start()
        sends.append(k)
    for i in range(8):
        forward(i)
    halos[2].wait_recv()
    halos[3].wait_recv()
    halo(xe.at[:, 48:64], xne, s)
    halo(xw.at[:, 48:64], xnw, s)
    halo(xe.at[:, 0:16], xse, n)
    halo(xw.at[:, 0:16], xsw, n)
    for i in range(8, 15):
        forward(i)
    halo(c_ref.at[:, 0:8], ce, w)
    halo(c_ref.at[:, 24:32], cw, e)
    halo(c_ref.at[29:32], cn, s)
    halo(c_ref.at[0:3], cs, n)
    for k in (0, 1, 4, 5, 6, 7):
        halos[k].wait_recv()
    for q in range(9):
        xf[q * PITCH + 8 : q * PITCH + 72, :] = xn[q + 1].astype(F32) * north
        xf[q * PITCH + 80 : q * PITCH + 96, :] = jnp.zeros((16, 128), F32)
    for q in range(10):
        xf[(q + 73) * PITCH + 8 : (q + 73) * PITCH + 72, :] = xs[q].astype(F32) * south
        xf[(q + 73) * PITCH + 80 : (q + 73) * PITCH + 96, :] = jnp.zeros((16, 128), F32)
    for j in range(10):
        for ref, rn, rs, ats in ((xe, xne, xse, (72 + j,)), (xw, xnw, xsw, (94 + j, j - 2))):
            mid = ref[j].astype(F32)
            top = rn[j].astype(F32)[7:16] * north
            low = rs[j].astype(F32)[0:10] * south
            for at in ats:
                if at >= 0:
                    xf[pl.ds(9 * PITCH + at, 64, stride=PITCH), :] = mid
                    xf[pl.ds(at, 9, stride=PITCH), :] = top
                    xf[pl.ds(73 * PITCH + at, 10, stride=PITCH), :] = low
    for i in range(15):
        share(i)
    def split(dst, p, idx):
        for k in range(3):
            dst[idx, :, 128 * k : 128 * k + 128] = xf[pl.ds(p * PITCH + 7 + k, W, stride=2), :].astype(BF16)
    def split_pair(k, _):
        split(x0, 2 * k, k)
        split(x1, 2 * k + 1, k)
        return 0
    lax.fori_loop(0, 41, split_pair, 0)
    split(x0, 82, 41)
    for half in range(2):
        for zz in range(ZS):
            q = half * 16 + zz * 2 + 1 - core
            remote(own, wb.at[q], psend.at[15], precv.at[q], (partner, lon)).wait_recv()

    for g in range(GROUPS):
        for k in range(XS):
            tr[56 * k : 56 * k + 56, :] = wb[g, k].astype(F32)
        at = 54 * g
        kf2[at : at + 54, 0:128] = tr[0:54, :]
        kf2[at : at + 54, 128:192] = tr[72:126, 0:64]
        kf3[at : at + 54, 0:64] = tr[72:126, 64:128]
        kf3[at : at + 54, 64:192] = tr[144:198, :]
        at = 36 * g
        kg[at : at + 18, 0:128] = tr[54:72, :]
        kg[at : at + 18, 128:192] = tr[126:144, 0:64]
        kg[at + 18 : at + 36, 0:64] = tr[126:144, 64:128]
        kg[at + 18 : at + 36, 64:192] = tr[198:216, :]
    k1[...] = kg[...].astype(BF16)
    k2[...] = kf2[...].astype(BF16)
    k3[...] = kf3[...].astype(BF16)

    def rows_ok(start, n, first):
        i = lax.broadcasted_iota(jnp.int32, (n, W, 192), 0) + (start + first)
        glob = i + 32 * lat
        return (glob >= 0) & (glob < 32 * (last + 1))
    def put_shifted(dst, start, n, value):
        dst[1, pl.ds(start, n)] = value.astype(BF16)
        dst[0, pl.ds(start, n)] = pltpu.roll(value, 1, 1).astype(BF16)
        dst[2, pl.ds(start, n)] = pltpu.roll(value, W - 1, 1).astype(BF16)
    def chunks(total, n, body, lo=0, hi=None):
        count = -(-total // n)
        def step(k, _):
            body(jnp.minimum(k * n, total - n))
            return 0
        lax.fori_loop(lo, count if hi is None else hi, step, 0)

    def h_one(s):
        n = 14
        acc = mm(x0[pl.ds(s, n)].reshape(n * W, 384), k1[0:384])
        acc += mm(x1[pl.ds(s, n)].reshape(n * W, 384), k1[384:768])
        acc += mm(x0[pl.ds(s + 1, n)].reshape(n * W, 384), k1[768:1152])
        put_shifted(hs1, s, n, jnp.where(rows_ok(s, n, -4), acc.reshape(n, W, 192), 0.0))
    chunks(41, 14, h_one)

    halos[8].wait_recv()
    halos[9].wait_recv()
    halo(ce.at[29:32], cne, s)
    halo(cw.at[29:32], cnw, s)
    halo(ce.at[0:3], cse, n)
    halo(cw.at[0:3], csw, n)

    def conv(src, k, s, n):
        acc = None
        for a in range(3):
            for b in range(3):
                t = mm(src[b, pl.ds(s + a, n)].reshape(n * W, 192), k[(3 * a + b) * 192 : (3 * a + b + 1) * 192])
                acc = t if acc is None else acc + t
        return acc.reshape(n, W, 192)
    def tconv(src, k, s, n):
        acc = None
        for a in range(3):
            for b in range(3):
                t = mmt(src[2 - b, pl.ds(s + 2 - a, n)].reshape(n * W, 192), k[(3 * a + b) * 192 : (3 * a + b + 1) * 192])
                acc = t if acc is None else acc + t
        return acc.reshape(n, W, 192)

    def h_two(s):
        n = 13
        v = conv(hs1, k2, s, n)
        p2[pl.ds(s, n)] = v
        h = v / (1.0 + jnp.exp(-v))
        put_shifted(hs2, s, n, jnp.where(rows_ok(s, n, -3), h, 0.0))
    chunks(39, 13, h_two)

    for k in halos[10:16]:
        k.wait_recv()
    def cot(idx, row, e, w):
        cf[idx, 0:32, :] = row.astype(F32)
        cf[idx, 32:40, :] = e.astype(F32)
        cf[idx, 40:48, :] = w.astype(F32)
    def cot_own(k, _):
        cot(k + 2, c_ref[k], ce[k], cw[k])
        return 0
    lax.fori_loop(0, 32, cot_own, 0)
    for q in range(2):
        cot(q, cn[q + 1], cne[q + 1], cnw[q + 1])
    for q in range(3):
        cot(q + 34, cs[q], cse[q], csw[q])

    def deriv(v):
        sg = 1.0 / (1.0 + jnp.exp(-v))
        return sg, sg * (1.0 + v * (1.0 - sg))
    def d_three(s):
        n = 13
        v = conv(hs2, k3, s, n)
        sg, dv = deriv(v)
        bs[1, pl.ds(s, n)] = (v * sg).astype(BF16)
        put_shifted(ds3, s, n, jnp.where(rows_ok(s, n, -2), cf[pl.ds(s, n)] * dv, 0.0))
    chunks(37, 13, d_three)
    feat_ref[...] = bs[1, 2:34, 0:32, :]

    def wgrad(src, off, dst):
        for a in range(3):
            for b in range(3):
                win = src[b, off + a : off + a + 32, 0:32, :].reshape(1024, 192)
                t = mm(dt[...], win)
                n0 = (3 * a + b) * 192
                dst[n0 : n0 + 192, :] = t.T
    def to_partner(i, g, a, r):
        rows, group = ROWS[i], 36 if i == 2 else 54
        for zz in range(ZS):
            for c in range(2):
                for q in range(XS):
                    for y in range(2):
                        base = (y * 16 + zz * 2 + c) * group + STARTS[i][q]
                        st[0:rows, 192 * y : 192 * y + 192] = g[base : base + rows, :]
                    a[zz, c, q] = st[0:rows, :].astype(BF16)
        k = remote(a.at[:, 1 - core], r, a_send.at[i], a_recv.at[i], (partner, lon))
        k.start()
        sends.append(k)
        return k
    def along_x(i, k, a, r, sx, qx, acc):
        k.wait_recv()
        for d in (2, 1, 3, 0):
            q = xq[d]
            total = a[:, core, q].astype(F32) + r[:, q].astype(F32)
            if d:
                sx[d] = total.astype(BF16)
                m = remote(sx.at[d], qx.at[x], x_send.at[i, d], x_recv.at[i, x], (lat, q * 2 + yl))
                m.start()
                sends.append(m)
            else:
                acc[...] = total
    def along_z(i, sx, qx, acc, tz, zb):
        for d in (1, 3, 2):
            q = xq[d]
            remote(sx.at[d], qx.at[q], x_send.at[i, d], x_recv.at[i, q], (lat, q * 2 + yl)).wait_recv()
        acc[...] = acc[...] + (qx[xq[1]].astype(F32) + qx[xq[3]].astype(F32)) + qx[xq[2]].astype(F32)
        for d in (4, 3, 5, 2, 6, 1, 7):
            zz = zs[d]
            tz[d] = acc[zz].astype(BF16)
            m = remote(tz.at[d], zb.at[z], z_send.at[i, d], z_recv.at[i, z], (lat_of(yh, zz), lon))
            m.start()
            sends.append(m)
    ys = [(1 - yh, yl, (across, lon)), (yh, 1 - yl, (lat, beside)), (1 - yh, 1 - yl, (across, beside))]
    def along_y(i, acc, tz, zb, u, f, l):
        size = S1 if i == 2 else S2
        total = acc[z]
        for d in near:
            zz = zs[d]
            remote(tz.at[d], zb.at[zz], z_send.at[i, d], z_recv.at[i, zz], (lat_of(yh, zz), lon)).wait_recv()
            total = total + zb[zz].astype(F32)
        u[...] = total
        def cut(shift):
            for y in range(2):
                for piece, lane, row, at, length in flat_moves(size, shift):
                    f[2 * y + piece, :, lane : lane + length] = u[row : row + 1, 192 * y + at : 192 * y + at + length]
        if i == 2:
            cut(0)
        else:
            @pl.when(lax.rem(x, 2) == 0)
            def _():
                cut(0)
            @pl.when(lax.rem(x, 2) == 1)
            def _():
                cut(96)
        me = 2 * yh + yl
        for d, (h, b, peer) in enumerate(ys):
            m = remote(f.at[2 * h + b], l.at[me], y_send.at[i, d], y_recv.at[i, me], peer)
            m.start()
            sends.append(m)
        l[me] = f[me]
    def total_of(i, f, l):
        for d, (h, b, peer) in enumerate(ys):
            remote(f.at[2 * h + b], l.at[2 * h + b], y_send.at[i, d], y_recv.at[i, 2 * h + b], peer).wait_recv()
        return (((l[0] + l[1]) + (l[2] + l[3])) * (1.0 / LOSS_CELLS)).reshape(S1 if i == 2 else S2)

    dt[...] = ds3[1, 2:34, 0:32, :].reshape(1024, 192).T
    wgrad(hs2, 2, g3)
    c3 = to_partner(0, g3, a3, r3)

    def d_two(s):
        n = 12
        v = tconv(ds3, k3, s, n)
        _, dv = deriv(p2[pl.ds(s + 2, n)])
        put_shifted(ds2, s, n, jnp.where(rows_ok(s, n, -1), v * dv, 0.0))
    chunks(35, 12, d_two)
    along_x(0, c3, a3, r3, s3, q3, acc3)
    dt[...] = ds2[1, 1:33, 0:32, :].reshape(1024, 192).T
    wgrad(hs1, 3, g2)
    c2 = to_partner(1, g2, a2, r2)

    def b_one(s):
        n = 11
        v = jnp.where(rows_ok(s, n, 0), tconv(ds2, k2, s, n), 0.0)
        bs[1, pl.ds(s, n)] = v.astype(BF16)
        bs[2, pl.ds(s, n)] = pltpu.roll(v, W - 1, 1).astype(BF16)
    chunks(33, 11, b_one, 0, 1)
    along_x(1, c2, a2, r2, s2, q2, acc2)
    chunks(33, 11, b_one, 1, 2)
    along_z(0, s3, q3, acc3, t3, z3)
    chunks(33, 11, b_one, 2, 3)
    dt[...] = bs[1, 0:32, 0:32, :].reshape(1024, 192).T
    for a in range(3):
        src = x1 if a == 1 else x0
        off = 4 + (a == 2)
        win = src[off : off + 32, 0:32, :].reshape(1024, 384)
        g1[384 * a : 384 * a + 384, :] = mm(dt[...], win).T
    c1 = to_partner(2, g1, a1, r1)
    along_z(1, s2, q2, acc2, t2, z2)
    def k1t(a, b):
        n0 = (3 * a + b) * 128
        return k1[n0 : n0 + 128]
    def gin(i):
        n = 8
        here = bs[1, pl.ds(i, n), 0:32, :].reshape(n * 32, 192)
        right = bs[2, pl.ds(i, n), 0:32, :].reshape(n * 32, 192)
        below = bs[1, pl.ds(i + 1, n), 0:32, :].reshape(n * 32, 192)
        corner = bs[2, pl.ds(i + 1, n), 0:32, :].reshape(n * 32, 192)
        ee = mmt(here, k1t(1, 1))
        eo = mmt(right, k1t(1, 0)) + mmt(here, k1t(1, 2))
        oe = mmt(below, k1t(0, 1)) + mmt(here, k1t(2, 1))
        oo = mmt(corner, k1t(0, 0)) + mmt(below, k1t(0, 2)) + mmt(right, k1t(2, 0)) + mmt(here, k1t(2, 2))
        il[pl.ds(0, n * 32, stride=2), :] = ee
        il[pl.ds(1, n * 32, stride=2), :] = eo
        il[pl.ds(n * 64, n * 32, stride=2), :] = oe
        il[pl.ds(n * 64 + 1, n * 32, stride=2), :] = oo
        even = il[0 : n * 64, :].reshape(n, 64, 128).astype(BF16)
        odd = il[n * 64 : n * 128, :].reshape(n, 64, 128).astype(BF16)
        for m in range(n):
            gin_ref[2 * (i + m)] = even[m]
            gin_ref[2 * (i + m) + 1] = odd[m]
    chunks(32, 8, gin, 0, 1)
    along_x(2, c1, a1, r1, s1, q1, acc1)
    chunks(32, 8, gin, 1, 4)
    along_y(0, acc3, t3, z3, u3, f3, l3)
    along_z(2, s1, q1, acc1, t1, z1)
    along_y(1, acc2, t2, z2, u2, f2, l2)
    o3[...] = total_of(0, f3, l3)
    o2[...] = total_of(1, f2, l2)
    along_y(2, acc1, t1, z1, u1, f1, l1)
    o1[...] = total_of(2, f1, l1)
    for k in sends:
        k.wait_send()


def level(w1, w2, w3, x, c):
    V, D = pltpu.VMEM, pltpu.SemaphoreType.DMA
    vm = pl.BlockSpec(memory_space=pltpu.VMEM)
    hbm = pl.BlockSpec(memory_space=pl.ANY)
    sds = jax.ShapeDtypeStruct
    def each(shape_of, dtype=BF16):
        return [V(shape_of(r), dtype) for r in ROWS]
    def flats():
        return [V((4, 1, n), F32) for n in (S2, S2, S1)]
    halos = [(10, 64, 128)] * 4 + [(10, 16, 128)] * 4 + [(32, 8, 192)] * 2 + [(3, 32, 192)] * 2 + [(3, 8, 192)] * 4
    return pl.pallas_call(
        level_kernel,
        out_shape=(sds((32, 32, 192), BF16), sds((64, 64, 128), BF16), sds((S1,), F32), sds((S2,), F32), sds((S2,), F32)),
        in_specs=[vm, vm, vm, hbm, hbm],
        out_specs=(vm,) * 5,
        scratch_shapes=[
            V((64, 64, 128), BF16), V((32, 32, 192), BF16), V((1, 3456), F32), V((LON, 1, 3456), F32), V((72, 384), F32),
            V((XS, 56, 128), BF16), V((2, 10, 64, 128), BF16), *[V(s, BF16) for s in halos],
            V((GROUPS, XS, 56, 128), BF16), V((224, 128), F32),
            V((83 * PITCH, 128), F32), V((42, W, 384), BF16), V((42, W, 384), BF16),
            V((1728, 192), F32), V((1728, 192), F32), V((1152, 192), F32),
            V((1152, 192), BF16), V((1728, 192), BF16), V((1728, 192), BF16),
            V((37, W, 192), F32), V((3, 41, W, 192), BF16), V((3, 39, W, 192), BF16),
            V((3, 37, W, 192), BF16), V((3, 35, W, 192), BF16), V((3, 37, W, 192), BF16),
            V((39, W, 192), F32), V((192, 1024), BF16), V((1152, 192), F32), V((1728, 192), F32), V((1728, 192), F32),
            V((14, 384), F32), V((1024, 128), F32),
            *each(lambda r: (ZS, 2, XS, r, 384)), *each(lambda r: (ZS, XS, r, 384)),
            *each(lambda r: (XS, ZS, r, 384)), *each(lambda r: (XS, ZS, r, 384)),
            *each(lambda r: (ZS, r, 384), F32), *each(lambda r: (ZS, r, 384)), *each(lambda r: (ZS, r, 384)),
            *each(lambda r: (r, 384), F32), *flats(), *flats(),
            D((2,)), D((LON,)), D((LON,)), D((20,)), D((20,)), D((16,)), D((GROUPS, XS)), D((16, XS)), D((16,)), D((GROUPS,)),
            D((3,)), D((3,)), D((3, XS)), D((3, XS)), D((3, ZS)), D((3, ZS)), D((3, 4)), D((3, 4)),
        ],
        compiler_params=pltpu.CompilerParams(collective_id=0, has_side_effects=True, vmem_limit_bytes=63 * 1024 * 1024),
        name="level",
    )(w1, w2, w3, x, c)


def finish_kernel(f, g, a, b, c, fo, go, ao, bo, co, fv, gv, av, bv, cv, isem, osem):
    trips = [(f, fv, fo), (a, av, ao), (b, bv, bo), (c, cv, co)]
    trips += [(g.at[16 * k : 16 * k + 16], gv.at[16 * k : 16 * k + 16], go.at[16 * k : 16 * k + 16]) for k in range(4)]
    ins = [pltpu.make_async_copy(src, mid, isem.at[i]) for i, (src, mid, _) in enumerate(trips)]
    outs = [pltpu.make_async_copy(mid, dst, osem.at[i]) for i, (_, mid, dst) in enumerate(trips)]
    for k in ins:
        k.start()
    for k, m in zip(ins, outs):
        k.wait()
        m.start()
    for m in outs:
        m.wait()


def finish(*arrays):
    hbm = pl.BlockSpec(memory_space=pl.ANY)
    return pl.pallas_call(
        finish_kernel,
        out_shape=tuple(jax.ShapeDtypeStruct(a.shape, a.dtype) for a in arrays),
        in_specs=[hbm] * 5,
        out_specs=(hbm,) * 5,
        scratch_shapes=[*[pltpu.VMEM(a.shape, a.dtype) for a in arrays],
                        pltpu.SemaphoreType.DMA((8,)), pltpu.SemaphoreType.DMA((8,))],
        name="results",
    )(*arrays)


def local(inputs, w_first, w_second, w_third, cotangent):
    return finish(*level(w_first, w_second, w_third, inputs, cotangent))


def solution(mesh):
    tile, flat = P("lat", "lon", None), P(("lat", "lon"))
    return jax.shard_map(
        local,
        mesh=mesh,
        in_specs=(tile, flat, flat, flat, tile),
        out_specs=(tile, tile, flat, flat, flat),
        check_vma=False,
    )
```

time: 104 us -> 87.2 us (0.84)
  Pallas kernels: 98.2 us -> 86.1 us
  local copies, waits for them, and re-layouts: 4.73 us -> 0 us
    pallas_call x1, Pallas kernels: 42.9 us -> 2.33 us  [finish(): pl.pallas_call(finish_kernel, out_shape=tuple((jax.ShapeDtypeStruct(a.sha...]
    pallas_call x1, Pallas kernels: 55.3 us -> 83.8 us  [level(): pl.pallas_call(level_kernel, out_shape=(sds((32, 32, 192), BF16), sds((64...]
    unnamed x13 -> x0, local copies, waits for them, and re-layouts: 4.73 us -> none
where the time goes in v3:
time: 87.2 us; the launch traced here: 86.9 us
  Pallas kernels  86.1 us (99%)
    pallas_call x1, Pallas kernels, level(): pl.pallas_call(level_kernel, out_shape=(sds((32, 32, 192), BF16), sds((64...  83.8 us
    pallas_call x1, Pallas kernels, finish(): pl.pallas_call(finish_kernel, out_shape=tuple((jax.ShapeDtypeStruct(a.sha...  2.33 us

profile of v3, /device:TPU:2, one launch (start us, length us, event | category | flops | bytes accessed | tf_op | source)
XLA Modules:
  0.0 86.9 jit_solution(4751916929797941300)
XLA Ops:
  0.6 83.8 %level.1 = (bf16[32,32,192]{2,1,0:T(8,128)(2,1)}, bf16[64,64,128]{2,1,0:T(8,128)(2,1)}, f32[864]{0:T(1024)}, f32[1296]{0:T(1024)}, f32[1296]{0:T(1024)}) custom-call(bf16[864]{0:T(1024)(128)(2,1)} %w1.1, bf16[1296]{0:T(1024)(128)(2,1)} %w2.1, bf16[1296]{0:T(1024)(128)(2,1)} %w3.1, bf16[64,64,128]{2,1,0:T(8,128)(2,1)} %x_hbm.1, bf16[32,32,192]{2,1,0:T(8,128)(2,1)} %c_hbm.1), custom_call_target="tpu_custom_call" | custom-call | tf_op jit(solution)/shard_map/level/pallas_call | solution.py:475
  84.4 2.3 %results.1 = (bf16[32,32,192]{2,1,0:T(8,128)(2,1)}, bf16[64,64,128]{2,1,0:T(8,128)(2,1)}, f32[864]{0:T(1024)}, f32[1296]{0:T(1024)}, f32[1296]{0:T(1024)}) custom-call(bf16[32,32,192]{2,1,0:T(8,128)(2,1)} %get-tuple-element.10.f, bf16[64,64,128]{2,1,0:T(8,128)(2,1)} %get-tuple-element.11.g, f32[864]{0:T(1024)} %get-tuple-element.12.a, ...), custom_call_target="tpu_custom_call" | custom-call | tf_op jit(solution)/shard_map/results/pallas_call | solution.py:519

commit v4 on v3

--- a/solution.py
+++ b/solution.py
@@ -14,6 +14,8 @@
 S1, S2 = 864, 1296
 XS = 4
 ROWS = (14, 14, 9)
+PACKED = (48, 48, 32)
+ORDER = (4, 3, 5, 2, 6, 1, 7, 0)
 STARTS = ((0, 13, 27, 40), (0, 13, 27, 40), (0, 9, 18, 27))
 
 
@@ -44,14 +46,16 @@
     return moves
 
 
-def flat_moves(size, shift):
+def flat_moves(size, shift, rows, y):
     out = []
     for piece in range(2):
         lane = 0
         while lane < size:
             at = shift + piece * size + lane
-            n = min(size - lane, 192 - at % 192)
-            out.append((piece, lane, at // 192, at % 192, n))
+            row, col = at // 192, at % 192
+            n = min(size - lane, (128 if col < 128 else 192) - col)
+            spot = (y * rows + row, col) if col < 128 else (2 * rows + row, 64 * y + col - 128)
+            out.append((piece, lane, *spot, n))
             lane += n
     return out
 
@@ -150,6 +154,11 @@
     sends.append(k)
     wb[lat] = own[...]
 
+    halo(c_ref.at[:, 0:8], ce, w)
+    halo(c_ref.at[:, 24:32], cw, e)
+    halo(c_ref.at[29:32], cn, s)
+    halo(c_ref.at[0:3], cs, n)
+
     north = (lat > 0).astype(F32)
     south = (lat < last).astype(F32)
     def own_row(r, _):
@@ -172,7 +181,7 @@
         k = remote(wb.at[q], wb.at[q], psend.at[i], precv.at[q], (partner, lon))
         k.start()
         sends.append(k)
-    for i in range(8):
+    for i in range(15):
         forward(i)
     halos[2].wait_recv()
     halos[3].wait_recv()
@@ -180,31 +189,12 @@
     halo(xw.at[:, 48:64], xnw, s)
     halo(xe.at[:, 0:16], xse, n)
     halo(xw.at[:, 0:16], xsw, n)
-    for i in range(8, 15):
-        forward(i)
-    halo(c_ref.at[:, 0:8], ce, w)
-    halo(c_ref.at[:, 24:32], cw, e)
-    halo(c_ref.at[29:32], cn, s)
-    halo(c_ref.at[0:3], cs, n)
-    for k in (0, 1, 4, 5, 6, 7):
-        halos[k].wait_recv()
-    for q in range(9):
-        xf[q * PITCH + 8 : q * PITCH + 72, :] = xn[q + 1].astype(F32) * north
-        xf[q * PITCH + 80 : q * PITCH + 96, :] = jnp.zeros((16, 128), F32)
-    for q in range(10):
-        xf[(q + 73) * PITCH + 8 : (q + 73) * PITCH + 72, :] = xs[q].astype(F32) * south
-        xf[(q + 73) * PITCH + 80 : (q + 73) * PITCH + 96, :] = jnp.zeros((16, 128), F32)
-    for j in range(10):
-        for ref, rn, rs, ats in ((xe, xne, xse, (72 + j,)), (xw, xnw, xsw, (94 + j, j - 2))):
-            mid = ref[j].astype(F32)
-            top = rn[j].astype(F32)[7:16] * north
-            low = rs[j].astype(F32)[0:10] * south
-            for at in ats:
-                if at >= 0:
-                    xf[pl.ds(9 * PITCH + at, 64, stride=PITCH), :] = mid
-                    xf[pl.ds(at, 9, stride=PITCH), :] = top
-                    xf[pl.ds(73 * PITCH + at, 10, stride=PITCH), :] = low
-    for i in range(15):
+    sides = [(xe, xne, xse, (72 + j,), j) for j in range(10)] + [(xw, xnw, xsw, (94 + j, j - 2), j) for j in range(10)]
+    for ref, rn, rs, ats, j in sides:
+        for at in ats:
+            if at >= 0:
+                xf[pl.ds(9 * PITCH + at, 64, stride=PITCH), :] = ref[j].astype(F32)
+    for i in range(5):
         share(i)
     def split(dst, p, idx):
         for k in range(3):
@@ -213,7 +203,28 @@
         split(x0, 2 * k, k)
         split(x1, 2 * k + 1, k)
         return 0
-    lax.fori_loop(0, 41, split_pair, 0)
+    lax.fori_loop(5, 36, split_pair, 0)
+    for i in range(5, 10):
+        share(i)
+    for k in (0, 1, 8, 9, 10, 11):
+        halos[k].wait_recv()
+    for q in range(9):
+        xf[q * PITCH + 8 : q * PITCH + 72, :] = xn[q + 1].astype(F32) * north
+        xf[q * PITCH + 80 : q * PITCH + 96, :] = jnp.zeros((16, 128), F32)
+    for q in range(10):
+        xf[(q + 73) * PITCH + 8 : (q + 73) * PITCH + 72, :] = xs[q].astype(F32) * south
+        xf[(q + 73) * PITCH + 80 : (q + 73) * PITCH + 96, :] = jnp.zeros((16, 128), F32)
+    for ref, rn, rs, ats, j in sides:
+        top = rn[j].astype(F32)[7:16] * north
+        low = rs[j].astype(F32)[0:10] * south
+        for at in ats:
+            if at >= 0:
+                xf[pl.ds(at, 9, stride=PITCH), :] = top
+                xf[pl.ds(73 * PITCH + at, 10, stride=PITCH), :] = low
+    for i in range(10, 15):
+        share(i)
+    lax.fori_loop(0, 5, split_pair, 0)
+    lax.fori_loop(36, 41, split_pair, 0)
     split(x0, 82, 41)
     for half in range(2):
         for zz in range(ZS):
@@ -260,8 +271,8 @@
         put_shifted(hs1, s, n, jnp.where(rows_ok(s, n, -4), acc.reshape(n, W, 192), 0.0))
     chunks(41, 14, h_one)
 
-    halos[8].wait_recv()
-    halos[9].wait_recv()
+    halos[4].wait_recv()
+    halos[5].wait_recv()
     halo(ce.at[29:32], cne, s)
     halo(cw.at[29:32], cnw, s)
     halo(ce.at[0:3], cse, n)
@@ -290,7 +301,7 @@
         put_shifted(hs2, s, n, jnp.where(rows_ok(s, n, -3), h, 0.0))
     chunks(39, 13, h_two)
 
-    for k in halos[10:16]:
+    for k in halos[6:8] + halos[12:16]:
         k.wait_recv()
     def cot(idx, row, e, w):
         cf[idx, 0:32, :] = row.astype(F32)
@@ -324,6 +335,7 @@
                 t = mm(dt[...], win)
                 n0 = (3 * a + b) * 192
                 dst[n0 : n0 + 192, :] = t.T
+    st[...] = jnp.zeros_like(st)
     def to_partner(i, g, a, r):
         rows, group = ROWS[i], 36 if i == 2 else 54
         for zz in range(ZS):
@@ -331,39 +343,50 @@
                 for q in range(XS):
                     for y in range(2):
                         base = (y * 16 + zz * 2 + c) * group + STARTS[i][q]
-                        st[0:rows, 192 * y : 192 * y + 192] = g[base : base + rows, :]
-                    a[zz, c, q] = st[0:rows, :].astype(BF16)
+                        st[y * rows : (y + 1) * rows, :] = g[base : base + rows, 0:128]
+                        st[2 * rows : 3 * rows, 64 * y : 64 * y + 64] = g[base : base + rows, 128:192]
+                    a[zz, c, q] = st[0 : PACKED[i], :].astype(BF16)
         k = remote(a.at[:, 1 - core], r, a_send.at[i], a_recv.at[i], (partner, lon))
         k.start()
         sends.append(k)
         return k
     def along_x(i, k, a, r, sx, qx, acc):
         k.wait_recv()
-        for d in (2, 1, 3, 0):
-            q = xq[d]
-            total = a[:, core, q].astype(F32) + r[:, q].astype(F32)
-            if d:
-                sx[d] = total.astype(BF16)
-                m = remote(sx.at[d], qx.at[x], x_send.at[i, d], x_recv.at[i, x], (lat, q * 2 + yl))
-                m.start()
-                sends.append(m)
-            else:
-                acc[...] = total
+        for half in range(2):
+            for d in (2, 1, 3, 0):
+                q = xq[d]
+                for p in range(4 * half, 4 * half + 4):
+                    zz = zs[ORDER[p]]
+                    total = a[zz, core, q].astype(F32) + r[zz, q].astype(F32)
+                    if d:
+                        sx[d, p] = total.astype(BF16)
+                    else:
+                        acc[p] = total
+                if d:
+                    part = pl.ds(4 * half, 4)
+                    m = remote(sx.at[d, part], qx.at[x, part], x_send.at[i, d, half], x_recv.at[i, x, half], (lat, q * 2 + yl))
+                    m.start()
+                    sends.append(m)
     def along_z(i, sx, qx, acc, tz, zb):
-        for d in (1, 3, 2):
-            q = xq[d]
-            remote(sx.at[d], qx.at[q], x_send.at[i, d], x_recv.at[i, q], (lat, q * 2 + yl)).wait_recv()
-        acc[...] = acc[...] + (qx[xq[1]].astype(F32) + qx[xq[3]].astype(F32)) + qx[xq[2]].astype(F32)
-        for d in (4, 3, 5, 2, 6, 1, 7):
-            zz = zs[d]
-            tz[d] = acc[zz].astype(BF16)
-            m = remote(tz.at[d], zb.at[z], z_send.at[i, d], z_recv.at[i, z], (lat_of(yh, zz), lon))
-            m.start()
-            sends.append(m)
+        for half in range(2):
+            part = pl.ds(4 * half, 4)
+            for d in (1, 3, 2):
+                q = xq[d]
+                remote(sx.at[d, part], qx.at[q, part], x_send.at[i, d, half], x_recv.at[i, q, half], (lat, q * 2 + yl)).wait_recv()
+            for p in range(4 * half, 4 * half + 4):
+                d = ORDER[p]
+                total = acc[p] + (qx[xq[1], p].astype(F32) + qx[xq[3], p].astype(F32)) + qx[xq[2], p].astype(F32)
+                if d:
+                    tz[d] = total.astype(BF16)
+                    m = remote(tz.at[d], zb.at[z], z_send.at[i, d], z_recv.at[i, z], (lat_of(yh, zs[d]), lon))
+                    m.start()
+                    sends.append(m)
+                else:
+                    acc[p] = total
     ys = [(1 - yh, yl, (across, lon)), (yh, 1 - yl, (lat, beside)), (1 - yh, 1 - yl, (across, beside))]
     def along_y(i, acc, tz, zb, u, f, l):
         size = S1 if i == 2 else S2
-        total = acc[z]
+        total = acc[7]
         for d in near:
             zz = zs[d]
             remote(tz.at[d], zb.at[zz], z_send.at[i, d], z_recv.at[i, zz], (lat_of(yh, zz), lon)).wait_recv()
@@ -371,8 +394,8 @@
         u[...] = total
         def cut(shift):
             for y in range(2):
-                for piece, lane, row, at, length in flat_moves(size, shift):
-                    f[2 * y + piece, :, lane : lane + length] = u[row : row + 1, 192 * y + at : 192 * y + at + length]
+                for piece, lane, row, at, length in flat_moves(size, shift, ROWS[i], y):
+                    f[2 * y + piece, :, lane : lane + length] = u[row : row + 1, at : at + length]
         if i == 2:
             cut(0)
         else:
@@ -451,8 +474,8 @@
     chunks(32, 8, gin, 0, 1)
     along_x(2, c1, a1, r1, s1, q1, acc1)
     chunks(32, 8, gin, 1, 4)
+    along_z(2, s1, q1, acc1, t1, z1)
     along_y(0, acc3, t3, z3, u3, f3, l3)
-    along_z(2, s1, q1, acc1, t1, z1)
     along_y(1, acc2, t2, z2, u2, f2, l2)
     o3[...] = total_of(0, f3, l3)
     o2[...] = total_of(1, f2, l2)
@@ -468,7 +491,7 @@
     hbm = pl.BlockSpec(memory_space=pl.ANY)
     sds = jax.ShapeDtypeStruct
     def each(shape_of, dtype=BF16):
-        return [V(shape_of(r), dtype) for r in ROWS]
+        return [V(shape_of(r), dtype) for r in PACKED]
     def flats():
         return [V((4, 1, n), F32) for n in (S2, S2, S1)]
     halos = [(10, 64, 128)] * 4 + [(10, 16, 128)] * 4 + [(32, 8, 192)] * 2 + [(3, 32, 192)] * 2 + [(3, 8, 192)] * 4
@@ -487,13 +510,13 @@
             V((37, W, 192), F32), V((3, 41, W, 192), BF16), V((3, 39, W, 192), BF16),
             V((3, 37, W, 192), BF16), V((3, 35, W, 192), BF16), V((3, 37, W, 192), BF16),
             V((39, W, 192), F32), V((192, 1024), BF16), V((1152, 192), F32), V((1728, 192), F32), V((1728, 192), F32),
-            V((14, 384), F32), V((1024, 128), F32),
-            *each(lambda r: (ZS, 2, XS, r, 384)), *each(lambda r: (ZS, XS, r, 384)),
-            *each(lambda r: (XS, ZS, r, 384)), *each(lambda r: (XS, ZS, r, 384)),
-            *each(lambda r: (ZS, r, 384), F32), *each(lambda r: (ZS, r, 384)), *each(lambda r: (ZS, r, 384)),
-            *each(lambda r: (r, 384), F32), *flats(), *flats(),
+            V((48, 128), F32), V((1024, 128), F32),
+            *each(lambda r: (ZS, 2, XS, r, 128)), *each(lambda r: (ZS, XS, r, 128)),
+            *each(lambda r: (XS, ZS, r, 128)), *each(lambda r: (XS, ZS, r, 128)),
+            *each(lambda r: (ZS, r, 128), F32), *each(lambda r: (ZS, r, 128)), *each(lambda r: (ZS, r, 128)),
+            *each(lambda r: (r, 128), F32), *flats(), *flats(),
             D((2,)), D((LON,)), D((LON,)), D((20,)), D((20,)), D((16,)), D((GROUPS, XS)), D((16, XS)), D((16,)), D((GROUPS,)),
-            D((3,)), D((3,)), D((3, XS)), D((3, XS)), D((3, ZS)), D((3, ZS)), D((3, 4)), D((3, 4)),
+            D((3,)), D((3,)), D((3, XS, 2)), D((3, XS, 2)), D((3, ZS)), D((3, ZS)), D((3, 4)), D((3, 4)),
         ],
         compiler_params=pltpu.CompilerParams(collective_id=0, has_side_effects=True, vmem_limit_bytes=63 * 1024 * 1024),
         name="level",

time: 87.2 us -> 86.5 us (level)
  no operation moved by 1% of the time
where the time goes in v4:
time: 86.5 us; the launch traced here: 86.4 us
  Pallas kernels  85.8 us (99%)
    pallas_call x1, Pallas kernels, level(): pl.pallas_call(level_kernel, out_shape=(sds((32, 32, 192), BF16), sds((64...  83.4 us
    pallas_call x1, Pallas kernels, finish(): pl.pallas_call(finish_kernel, out_shape=tuple((jax.ShapeDtypeStruct(a.sha...  2.33 us

profile of v4, /device:TPU:2, one launch (start us, length us, event | category | flops | bytes accessed | tf_op | source)
XLA Modules:
  0.0 86.4 jit_solution(16521483205421832912)
XLA Ops:
  0.6 83.4 %level.1 = (bf16[32,32,192]{2,1,0:T(8,128)(2,1)}, bf16[64,64,128]{2,1,0:T(8,128)(2,1)}, f32[864]{0:T(1024)}, f32[1296]{0:T(1024)}, f32[1296]{0:T(1024)}) custom-call(bf16[864]{0:T(1024)(128)(2,1)} %w1.1, bf16[1296]{0:T(1024)(128)(2,1)} %w2.1, bf16[1296]{0:T(1024)(128)(2,1)} %w3.1, bf16[64,64,128]{2,1,0:T(8,128)(2,1)} %x_hbm.1, bf16[32,32,192]{2,1,0:T(8,128)(2,1)} %c_hbm.1), custom_call_target="tpu_custom_call" | custom-call | tf_op jit(solution)/shard_map/level/pallas_call | solution.py:498
  84.1 2.3 %results.1 = (bf16[32,32,192]{2,1,0:T(8,128)(2,1)}, bf16[64,64,128]{2,1,0:T(8,128)(2,1)}, f32[864]{0:T(1024)}, f32[1296]{0:T(1024)}, f32[1296]{0:T(1024)}) custom-call(bf16[32,32,192]{2,1,0:T(8,128)(2,1)} %get-tuple-element.10.f, bf16[64,64,128]{2,1,0:T(8,128)(2,1)} %get-tuple-element.11.g, f32[864]{0:T(1024)} %get-tuple-element.12.a, ...), custom_call_target="tpu_custom_call" | custom-call | tf_op jit(solution)/shard_map/results/pallas_call | solution.py:542

commit v5 on v4

--- a/solution.py
+++ b/solution.py
@@ -504,7 +504,7 @@
             V((64, 64, 128), BF16), V((32, 32, 192), BF16), V((1, 3456), F32), V((LON, 1, 3456), F32), V((72, 384), F32),
             V((XS, 56, 128), BF16), V((2, 10, 64, 128), BF16), *[V(s, BF16) for s in halos],
             V((GROUPS, XS, 56, 128), BF16), V((224, 128), F32),
-            V((83 * PITCH, 128), F32), V((42, W, 384), BF16), V((42, W, 384), BF16),
+            V((90 * PITCH, 128), F32), V((42, W, 384), BF16), V((42, W, 384), BF16),
             V((1728, 192), F32), V((1728, 192), F32), V((1152, 192), F32),
             V((1152, 192), BF16), V((1728, 192), BF16), V((1728, 192), BF16),
             V((37, W, 192), F32), V((3, 41, W, 192), BF16), V((3, 39, W, 192), BF16),

time: 86.5 us -> 86.5 us (level)
  no operation moved by 1% of the time
where the time goes in v5:
time: 86.5 us; the launch traced here: 86.4 us
  Pallas kernels  85.8 us (99%)
    pallas_call x1, Pallas kernels, level(): pl.pallas_call(level_kernel, out_shape=(sds((32, 32, 192), BF16), sds((64...  83.4 us
    pallas_call x1, Pallas kernels, finish(): pl.pallas_call(finish_kernel, out_shape=tuple((jax.ShapeDtypeStruct(a.sha...  2.33 us

profile of v5, /device:TPU:2, one launch (start us, length us, event | category | flops | bytes accessed | tf_op | source)
XLA Modules:
  0.0 86.4 jit_solution(17536512140707966776)
XLA Ops:
  0.6 83.4 %level.1 = (bf16[32,32,192]{2,1,0:T(8,128)(2,1)}, bf16[64,64,128]{2,1,0:T(8,128)(2,1)}, f32[864]{0:T(1024)}, f32[1296]{0:T(1024)}, f32[1296]{0:T(1024)}) custom-call(bf16[864]{0:T(1024)(128)(2,1)} %w1.1, bf16[1296]{0:T(1024)(128)(2,1)} %w2.1, bf16[1296]{0:T(1024)(128)(2,1)} %w3.1, bf16[64,64,128]{2,1,0:T(8,128)(2,1)} %x_hbm.1, bf16[32,32,192]{2,1,0:T(8,128)(2,1)} %c_hbm.1), custom_call_target="tpu_custom_call" | custom-call | tf_op jit(solution)/shard_map/level/pallas_call | solution.py:498
  84.1 2.3 %results.1 = (bf16[32,32,192]{2,1,0:T(8,128)(2,1)}, bf16[64,64,128]{2,1,0:T(8,128)(2,1)}, f32[864]{0:T(1024)}, f32[1296]{0:T(1024)}, f32[1296]{0:T(1024)}) custom-call(bf16[32,32,192]{2,1,0:T(8,128)(2,1)} %get-tuple-element.10.f, bf16[64,64,128]{2,1,0:T(8,128)(2,1)} %get-tuple-element.11.g, f32[864]{0:T(1024)} %get-tuple-element.12.a, ...), custom_call_target="tpu_custom_call" | custom-call | tf_op jit(solution)/shard_map/results/pallas_call | solution.py:542

commit v6 on v5

--- a/solution.py
+++ b/solution.py
@@ -154,10 +154,6 @@
     sends.append(k)
     wb[lat] = own[...]
 
-    halo(c_ref.at[:, 0:8], ce, w)
-    halo(c_ref.at[:, 24:32], cw, e)
-    halo(c_ref.at[29:32], cn, s)
-    halo(c_ref.at[0:3], cs, n)
 
     north = (lat > 0).astype(F32)
     south = (lat < last).astype(F32)
@@ -206,7 +202,7 @@
     lax.fori_loop(5, 36, split_pair, 0)
     for i in range(5, 10):
         share(i)
-    for k in (0, 1, 8, 9, 10, 11):
+    for k in (0, 1, 4, 5, 6, 7):
         halos[k].wait_recv()
     for q in range(9):
         xf[q * PITCH + 8 : q * PITCH + 72, :] = xn[q + 1].astype(F32) * north
@@ -223,6 +219,10 @@
                 xf[pl.ds(73 * PITCH + at, 10, stride=PITCH), :] = low
     for i in range(10, 15):
         share(i)
+    halo(c_ref.at[:, 0:8], ce, w)
+    halo(c_ref.at[:, 24:32], cw, e)
+    halo(c_ref.at[29:32], cn, s)
+    halo(c_ref.at[0:3], cs, n)
     lax.fori_loop(0, 5, split_pair, 0)
     lax.fori_loop(36, 41, split_pair, 0)
     split(x0, 82, 41)
@@ -271,13 +271,6 @@
         put_shifted(hs1, s, n, jnp.where(rows_ok(s, n, -4), acc.reshape(n, W, 192), 0.0))
     chunks(41, 14, h_one)
 
-    halos[4].wait_recv()
-    halos[5].wait_recv()
-    halo(ce.at[29:32], cne, s)
-    halo(cw.at[29:32], cnw, s)
-    halo(ce.at[0:3], cse, n)
-    halo(cw.at[0:3], csw, n)
-
     def conv(src, k, s, n):
         acc = None
         for a in range(3):
@@ -299,9 +292,16 @@
         p2[pl.ds(s, n)] = v
         h = v / (1.0 + jnp.exp(-v))
         put_shifted(hs2, s, n, jnp.where(rows_ok(s, n, -3), h, 0.0))
-    chunks(39, 13, h_two)
-
-    for k in halos[6:8] + halos[12:16]:
+    chunks(39, 13, h_two, 0, 2)
+    halos[8].wait_recv()
+    halos[9].wait_recv()
+    halo(ce.at[29:32], cne, s)
+    halo(cw.at[29:32], cnw, s)
+    halo(ce.at[0:3], cse, n)
+    halo(cw.at[0:3], csw, n)
+    chunks(39, 13, h_two, 2, 3)
+
+    for k in halos[10:16]:
         k.wait_recv()
     def cot(idx, row, e, w):
         cf[idx, 0:32, :] = row.astype(F32)

time: 86.5 us -> 86.6 us (level)
  no operation moved by 1% of the time
where the time goes in v6:
time: 86.6 us; the launch traced here: 86.5 us
  Pallas kernels  85.7 us (99%)
    pallas_call x1, Pallas kernels, level(): pl.pallas_call(level_kernel, out_shape=(sds((32, 32, 192), BF16), sds((64...  83.4 us
    pallas_call x1, Pallas kernels, finish(): pl.pallas_call(finish_kernel, out_shape=tuple((jax.ShapeDtypeStruct(a.sha...  2.33 us

profile of v6, /device:TPU:2, one launch (start us, length us, event | category | flops | bytes accessed | tf_op | source)
XLA Modules:
  0.0 86.5 jit_solution(17847746386728189508)
XLA Ops:
  0.6 83.4 %level.1 = (bf16[32,32,192]{2,1,0:T(8,128)(2,1)}, bf16[64,64,128]{2,1,0:T(8,128)(2,1)}, f32[864]{0:T(1024)}, f32[1296]{0:T(1024)}, f32[1296]{0:T(1024)}) custom-call(bf16[864]{0:T(1024)(128)(2,1)} %w1.1, bf16[1296]{0:T(1024)(128)(2,1)} %w2.1, bf16[1296]{0:T(1024)(128)(2,1)} %w3.1, bf16[64,64,128]{2,1,0:T(8,128)(2,1)} %x_hbm.1, bf16[32,32,192]{2,1,0:T(8,128)(2,1)} %c_hbm.1), custom_call_target="tpu_custom_call" | custom-call | tf_op jit(solution)/shard_map/level/pallas_call | solution.py:498
  84.0 2.3 %results.1 = (bf16[32,32,192]{2,1,0:T(8,128)(2,1)}, bf16[64,64,128]{2,1,0:T(8,128)(2,1)}, f32[864]{0:T(1024)}, f32[1296]{0:T(1024)}, f32[1296]{0:T(1024)}) custom-call(bf16[32,32,192]{2,1,0:T(8,128)(2,1)} %get-tuple-element.10.f, bf16[64,64,128]{2,1,0:T(8,128)(2,1)} %get-tuple-element.11.g, f32[864]{0:T(1024)} %get-tuple-element.12.a, ...), custom_call_target="tpu_custom_call" | custom-call | tf_op jit(solution)/shard_map/results/pallas_call | solution.py:542
